TPU v7x, 256 devices: a whole 4x4x8 slice. The times are simulated.
256 devices in a mesh: tm: 16 (over z, x_lo), gx: 8 (over y, core), gy: 2 (over x_hi).
Axes of the slice: x: 4 (x_hi: 2, x_lo: 2; x = x_hi * 2 + x_lo), y: 4, z: 8, core: 2. Of those that a mesh axis runs over, the one named last changes fastest.
Arguments:
- start_field: float32 [3, 4, 512, 512], P(None, None, 'gx', 'gy'), may hold values from -1 to 1, as said below
- demag_field: float32 [3, 4, 512, 512], P(None, None, 'gx', 'gy'), may hold values from -3 to 3
- region_map: int32 [4, 512, 512], P(None, 'gx', 'gy'), may hold values from 0 to 3
- material_table: float32 [4, 3], replicated, may hold values from 0.3 to 1.2
Outputs:
- end_states: float32 [16, 3, 4, 512, 512], P('tm', None, None, 'gx', 'gy')
- predicted_states: float32 [16, 3, 4, 512, 512], P('tm', None, None, 'gx', 'gy')
Inputs may be any that keep to these rules, and one draw needn't show every extreme that they name: `start_field`: every cell's vector has length at most 1.
All inputs are finite; a program needn't handle non-finite values.
Results may differ from a plain program's by a relative error of at most 0.00002.
Values sent between devices are 32-bit elements; how exact they have to be, the bound alone decides.
A program may use at most 64 MiB of HBM per device.

v0:
```python
import jax
import jax.numpy as jnp
from jax import lax
from jax.sharding import PartitionSpec as P

ITERS = 4


damping = 0.5
slice_length = 0.05


def padded_2(cells, sides, width):
    for axis, dim in sides:
        count = lax.axis_size(axis)
        head = lax.slice_in_dim(cells, 0, width, axis=dim)
        tail = lax.slice_in_dim(cells, cells.shape[dim] - width, cells.shape[dim], axis=dim)
        cells = jnp.concatenate(
            [
                lax.ppermute(tail, axis, [(i, (i + 1) % count) for i in range(count)]),
                cells,
                lax.ppermute(head, axis, [((i + 1) % count, i) for i in range(count)]),
            ],
            axis=dim,
        )
    return cells


def passed_along(value, axis, steps):
    count = lax.axis_size(axis)
    initial, last = (max(0, -steps), min(count, count - steps))
    return lax.ppermute(value, axis, [(source, source + steps) for source in range(initial, last)])


def cross(left, right):
    return jnp.stack(
        [
            left[1] * right[2] - left[2] * right[1],
            left[2] * right[0] - left[0] * right[2],
            left[0] * right[1] - left[1] * right[0],
        ]
    )


def rate(center, x_next, x_prev, y_next, y_prev, exchange, chirality, anisotropy, demag):
    z_next = jnp.concatenate([center[:, 1:], center[:, -1:]], axis=1)
    z_prev = jnp.concatenate([center[:, :1], center[:, :-1]], axis=1)
    laplace = x_next + x_prev + y_next + y_prev + z_next + z_prev - 6.0 * center
    slope_x = 0.5 * (x_next - x_prev)
    slope_y = 0.5 * (y_next - y_prev)
    field_x = exchange * laplace[0] + chirality * slope_x[2] + demag[0]
    field_y = exchange * laplace[1] + chirality * slope_y[2] + demag[1]
    field_z = (
        exchange * laplace[2]
        - chirality * (slope_x[0] + slope_y[1])
        + 2.0 * anisotropy * center[2]
        + demag[2]
    )
    field = jnp.stack([field_x, field_y, field_z])
    torque = cross(center, field)
    return -torque - damping * cross(center, torque)


def extend(field):
    return padded_2(field, (("gx", 2), ("gy", 3)), 1)


def padded_rate(padded, exchange, chirality, anisotropy, demag):
    center = padded[:, :, 1:-1, 1:-1]
    return rate(
        center,
        padded[:, :, 2:, 1:-1],
        padded[:, :, :-2, 1:-1],
        padded[:, :, 1:-1, 2:],
        padded[:, :, 1:-1, :-2],
        exchange,
        chirality,
        anisotropy,
        demag,
    )


def on_device(start_field, demag_field, region_map, material_table):
    columns = []
    for column in range(3):
        total = jnp.zeros(region_map.shape, jnp.float32)
        for klass in range(material_table.shape[0]):
            total = (
                total + (region_map == klass).astype(jnp.float32) * material_table[klass, column]
            )
        columns.append(total)
    exchange, chirality, anisotropy = columns
    half = 0.5 * slice_length

    def evaluate(padded):
        return padded_rate(padded, exchange, chirality, anisotropy, demag_field)

    slice_count = lax.axis_size("tm")
    position = lax.axis_index("tm")
    is_first = position == 0

    def advance(step_index, current):
        advanced = current + slice_length * evaluate(extend(current))
        incoming = passed_along(advanced, "tm", 1)
        return jnp.where(is_first, start_field, incoming)

    predicted = lax.fori_loop(0, slice_count - 1, advance, start_field)
    padded_guess = extend(predicted)
    first_rate = evaluate(padded_guess)
    nodes = [predicted, predicted, predicted]
    rates = [first_rate, first_rate, first_rate]
    padded_end = padded_guess
    node_two = predicted
    for sweep_index in range(ITERS):
        if sweep_index == 0:
            begin_padded = padded_guess
            rate_zero = first_rate
        else:
            incoming = passed_along(nodes[2], "tm", 1)
            begin_padded = extend(jnp.where(is_first, start_field, incoming))
            rate_zero = evaluate(begin_padded)
        begin = begin_padded[:, :, 1:-1, 1:-1]
        node_one = (
            begin
            + half * (rate_zero - rates[0])
            + slice_length * (5.0 / 24.0 * rates[0] + 1.0 / 3.0 * rates[1] - 1.0 / 24.0 * rates[2])
        )
        rate_one = evaluate(extend(node_one))
        node_two = (
            node_one
            + half * (rate_one - rates[1])
            + slice_length * (-1.0 / 24.0 * rates[0] + 1.0 / 3.0 * rates[1] + 5.0 / 24.0 * rates[2])
        )
        if sweep_index + 1 < ITERS:
            padded_end = extend(node_two)
            rate_two = evaluate(padded_end)
            nodes = [begin, node_one, node_two]
            rates = [rate_zero, rate_one, rate_two]
    return (node_two[None], predicted[None])


def solution(mesh):
    placed = (P(None, None, "gx", "gy"), P(None, None, "gx", "gy"), P(None, "gx", "gy"), P())
    return jax.shard_map(
        on_device,
        mesh=mesh,
        in_specs=placed,
        out_specs=(P("tm", None, None, "gx", "gy"), P("tm", None, None, "gx", "gy")),
        check_vma=False,
    )
```

profile of v0, /device:TPU:159, one launch (start us, length us, event | category | flops | bytes accessed | tf_op | source)
XLA Modules:
  0.0 1184.0 jit_solution(14225866562847420649)
XLA Ops:
  11.3 793.8 %while.10 = (s32[]{:T(128)}, f32[3,4,64,256]{3,2,1,0:T(8,128)S(1)}, pred[]{:T(512)}, f32[4,64,256]{2,1,0:T(8,128)S(1)}, f32[4,64,256]{2,1,0:T(8,128)S(1)}, /*ind...) while((s32[]{:T(128)}, f32[3,4,64,256]{3,2,1,0:T(8,128)S(1)}, ...), condition=%wide.region_1.2_spmd, body=%wide.region_0.1_spmd.sunk | while | flops 10301442 | bytes 31229760 | solution.py:107
  45.1 17.8 %collective-permute-done.4 = f32[3,4,64,256]{3,2,1,0:T(8,128)S(1)} collective-permute-done((f32[3,4,64,256]{3,2,1,0:T(8,128)}, f32[3,4,64,256]{3,2,1,0:T(8,128)S(1)}, u32[]{:S(2)}, u32[]{:S(2)}) %collective-permute-start.4) | collective-permute-done | bytes 786464 | tf_op jit(solution)/shard_map/while/body/eval_jaxpr/ppermute | solution.py:32
  99.4 17.9 %collective-permute-done.4 = f32[3,4,64,256]{3,2,1,0:T(8,128)S(1)} collective-permute-done((f32[3,4,64,256]{3,2,1,0:T(8,128)}, f32[3,4,64,256]{3,2,1,0:T(8,128)S(1)}, u32[]{:S(2)}, u32[]{:S(2)}) %collective-permute-start.4) | collective-permute-done | bytes 786464 | tf_op jit(solution)/shard_map/while/body/eval_jaxpr/ppermute | solution.py:32
  152.5 18.5 %collective-permute-done.4 = f32[3,4,64,256]{3,2,1,0:T(8,128)S(1)} collective-permute-done((f32[3,4,64,256]{3,2,1,0:T(8,128)}, f32[3,4,64,256]{3,2,1,0:T(8,128)S(1)}, u32[]{:S(2)}, u32[]{:S(2)}) %collective-permute-start.4) | collective-permute-done | bytes 786464 | tf_op jit(solution)/shard_map/while/body/eval_jaxpr/ppermute | solution.py:32
  204.5 18.8 %collective-permute-done.4 = f32[3,4,64,256]{3,2,1,0:T(8,128)S(1)} collective-permute-done((f32[3,4,64,256]{3,2,1,0:T(8,128)}, f32[3,4,64,256]{3,2,1,0:T(8,128)S(1)}, u32[]{:S(2)}, u32[]{:S(2)}) %collective-permute-start.4) | collective-permute-done | bytes 786464 | tf_op jit(solution)/shard_map/while/body/eval_jaxpr/ppermute | solution.py:32
  256.2 18.2 %collective-permute-done.4 = f32[3,4,64,256]{3,2,1,0:T(8,128)S(1)} collective-permute-done((f32[3,4,64,256]{3,2,1,0:T(8,128)}, f32[3,4,64,256]{3,2,1,0:T(8,128)S(1)}, u32[]{:S(2)}, u32[]{:S(2)}) %collective-permute-start.4) | collective-permute-done | bytes 786464 | tf_op jit(solution)/shard_map/while/body/eval_jaxpr/ppermute | solution.py:32
  290.7 10.8 collective-permute-done.2
  312.0 18.8 %collective-permute-done.4 = f32[3,4,64,256]{3,2,1,0:T(8,128)S(1)} collective-permute-done((f32[3,4,64,256]{3,2,1,0:T(8,128)}, f32[3,4,64,256]{3,2,1,0:T(8,128)S(1)}, u32[]{:S(2)}, u32[]{:S(2)}) %collective-permute-start.4) | collective-permute-done | bytes 786464 | tf_op jit(solution)/shard_map/while/body/eval_jaxpr/ppermute | solution.py:32
  363.1 18.4 %collective-permute-done.4 = f32[3,4,64,256]{3,2,1,0:T(8,128)S(1)} collective-permute-done((f32[3,4,64,256]{3,2,1,0:T(8,128)}, f32[3,4,64,256]{3,2,1,0:T(8,128)S(1)}, u32[]{:S(2)}, u32[]{:S(2)}) %collective-permute-start.4) | collective-permute-done | bytes 786464 | tf_op jit(solution)/shard_map/while/body/eval_jaxpr/ppermute | solution.py:32
  393.1 10.8 collective-permute-done.2
  413.8 18.7 %collective-permute-done.4 = f32[3,4,64,256]{3,2,1,0:T(8,128)S(1)} collective-permute-done((f32[3,4,64,256]{3,2,1,0:T(8,128)}, f32[3,4,64,256]{3,2,1,0:T(8,128)S(1)}, u32[]{:S(2)}, u32[]{:S(2)}) %collective-permute-start.4) | collective-permute-done | bytes 786464 | tf_op jit(solution)/shard_map/while/body/eval_jaxpr/ppermute | solution.py:32
  443.7 10.7 collective-permute-done.2
  464.9 19.2 %collective-permute-done.4 = f32[3,4,64,256]{3,2,1,0:T(8,128)S(1)} collective-permute-done((f32[3,4,64,256]{3,2,1,0:T(8,128)}, f32[3,4,64,256]{3,2,1,0:T(8,128)S(1)}, u32[]{:S(2)}, u32[]{:S(2)}) %collective-permute-start.4) | collective-permute-done | bytes 786464 | tf_op jit(solution)/shard_map/while/body/eval_jaxpr/ppermute | solution.py:32
  516.4 18.0 %collective-permute-done.4 = f32[3,4,64,256]{3,2,1,0:T(8,128)S(1)} collective-permute-done((f32[3,4,64,256]{3,2,1,0:T(8,128)}, f32[3,4,64,256]{3,2,1,0:T(8,128)S(1)}, u32[]{:S(2)}, u32[]{:S(2)}) %collective-permute-start.4) | collective-permute-done | bytes 786464 | tf_op jit(solution)/shard_map/while/body/eval_jaxpr/ppermute | solution.py:32
  566.9 17.2 %collective-permute-done.4 = f32[3,4,64,256]{3,2,1,0:T(8,128)S(1)} collective-permute-done((f32[3,4,64,256]{3,2,1,0:T(8,128)}, f32[3,4,64,256]{3,2,1,0:T(8,128)S(1)}, u32[]{:S(2)}, u32[]{:S(2)}) %collective-permute-start.4) | collective-permute-done | bytes 786464 | tf_op jit(solution)/shard_map/while/body/eval_jaxpr/ppermute | solution.py:32
  618.6 16.2 %collective-permute-done.4 = f32[3,4,64,256]{3,2,1,0:T(8,128)S(1)} collective-permute-done((f32[3,4,64,256]{3,2,1,0:T(8,128)}, f32[3,4,64,256]{3,2,1,0:T(8,128)S(1)}, u32[]{:S(2)}, u32[]{:S(2)}) %collective-permute-start.4) | collective-permute-done | bytes 786464 | tf_op jit(solution)/shard_map/while/body/eval_jaxpr/ppermute | solution.py:32
  670.3 17.0 %collective-permute-done.4 = f32[3,4,64,256]{3,2,1,0:T(8,128)S(1)} collective-permute-done((f32[3,4,64,256]{3,2,1,0:T(8,128)}, f32[3,4,64,256]{3,2,1,0:T(8,128)S(1)}, u32[]{:S(2)}, u32[]{:S(2)}) %collective-permute-start.4) | collective-permute-done | bytes 786464 | tf_op jit(solution)/shard_map/while/body/eval_jaxpr/ppermute | solution.py:32
  722.0 24.6 %collective-permute-done.4 = f32[3,4,64,256]{3,2,1,0:T(8,128)S(1)} collective-permute-done((f32[3,4,64,256]{3,2,1,0:T(8,128)}, f32[3,4,64,256]{3,2,1,0:T(8,128)S(1)}, u32[]{:S(2)}, u32[]{:S(2)}) %collective-permute-start.4) | collective-permute-done | bytes 786464 | tf_op jit(solution)/shard_map/while/body/eval_jaxpr/ppermute | solution.py:32
  756.5 10.7 collective-permute-done.2
  780.3 22.6 %collective-permute-done.4 = f32[3,4,64,256]{3,2,1,0:T(8,128)S(1)} collective-permute-done((f32[3,4,64,256]{3,2,1,0:T(8,128)}, f32[3,4,64,256]{3,2,1,0:T(8,128)S(1)}, u32[]{:S(2)}, u32[]{:S(2)}) %collective-permute-start.4) | collective-permute-done | bytes 786464 | tf_op jit(solution)/shard_map/while/body/eval_jaxpr/ppermute | solution.py:32
  812.9 10.7 collective-permute-done.8
  874.9 26.3 %collective-permute-done.21 = f32[3,4,66,1]{3,2,1,0:T(8,128)S(1)} collective-permute-done((f32[3,4,66,1]{3,2,1,0:T(8,128)S(1)}, f32[3,4,66,1]{3,2,1,0:T(8,128)S(1)}, u32[]{:S(2)}, u32[]{:S(2)}) %collective-permute-start.21) | collective-permute-done | bytes 3200 | tf_op jit(solution)/shard_map/ppermute | solution.py:20
  982.4 22.7 %collective-permute-done.34 = f32[3,4,66,1]{3,2,1,0:T(8,128)S(1)} collective-permute-done((f32[3,4,66,1]{3,2,1,0:T(8,128)S(1)}, f32[3,4,66,1]{3,2,1,0:T(8,128)S(1)}, u32[]{:S(2)}, u32[]{:S(2)}) %collective-permute-start.34) | collective-permute-done | bytes 3200 | tf_op jit(solution)/shard_map/ppermute | solution.py:20
  1087.0 24.0 %collective-permute-done.47 = f32[3,4,66,1]{3,2,1,0:T(8,128)S(1)} collective-permute-done((f32[3,4,66,1]{3,2,1,0:T(8,128)S(1)}, f32[3,4,66,1]{3,2,1,0:T(8,128)S(1)}, u32[]{:S(2)}, u32[]{:S(2)}) %collective-permute-start.47) | collective-permute-done | bytes 3200 | tf_op jit(solution)/shard_map/ppermute | solution.py:20
  (565 shorter events, 772.1 us)
Async XLA Ops:
  17.1 21.9 %collective-permute-start.3 = (f32[3,4,66,1]{3,2,1,0:T(8,128)S(1)}, f32[3,4,66,1]{3,2,1,0:T(8,128)S(1)}, u32[]{:S(2)}, u32[]{:S(2)}) collective-permute-start(f32[3,4,66,1]{3,2,1,0:T(8,128)S(1)} %get-tuple-element.360), channel_id=1, source_target_pairs={{0,1},{1,0},{2,3},{3,2},{4,5},{5,4},{6,7},{7,6},{8,9},{9,8},{10,11... | collective-permute-start | bytes 9512 | tf_op jit(solution)/shard_map/while/body/eval_jaxpr/ppermute | solution.py:20
  70.9 21.5 %collective-permute-start.3 = (f32[3,4,66,1]{3,2,1,0:T(8,128)S(1)}, f32[3,4,66,1]{3,2,1,0:T(8,128)S(1)}, u32[]{:S(2)}, u32[]{:S(2)}) collective-permute-start(f32[3,4,66,1]{3,2,1,0:T(8,128)S(1)} %get-tuple-element.360), channel_id=1, source_target_pairs={{0,1},{1,0},{2,3},{3,2},{4,5},{5,4},{6,7},{7,6},{8,9},{9,8},{10,11... | collective-permute-start | bytes 9512 | tf_op jit(solution)/shard_map/while/body/eval_jaxpr/ppermute | solution.py:20
  95.6 21.7 %collective-permute-start.4 = (f32[3,4,64,256]{3,2,1,0:T(8,128)}, f32[3,4,64,256]{3,2,1,0:T(8,128)S(1)}, u32[]{:S(2)}, u32[]{:S(2)}) collective-permute-start(f32[3,4,64,256]{3,2,1,0:T(8,128)} %fusion.306), channel_id=1, source_target_pairs={{0,16},{16,32},{32,48},{48,64},{64,80},{80,96},{96,112},{112,128},... | collective-permute-start | bytes 2359304 | tf_op jit(solution)/shard_map/while/body/eval_jaxpr/ppermute | solution.py:32
  125.0 21.5 %collective-permute-start.3 = (f32[3,4,66,1]{3,2,1,0:T(8,128)S(1)}, f32[3,4,66,1]{3,2,1,0:T(8,128)S(1)}, u32[]{:S(2)}, u32[]{:S(2)}) collective-permute-start(f32[3,4,66,1]{3,2,1,0:T(8,128)S(1)} %get-tuple-element.360), channel_id=1, source_target_pairs={{0,1},{1,0},{2,3},{3,2},{4,5},{5,4},{6,7},{7,6},{8,9},{9,8},{10,11... | collective-permute-start | bytes 9512 | tf_op jit(solution)/shard_map/while/body/eval_jaxpr/ppermute | solution.py:20
  149.6 21.3 %collective-permute-start.4 = (f32[3,4,64,256]{3,2,1,0:T(8,128)}, f32[3,4,64,256]{3,2,1,0:T(8,128)S(1)}, u32[]{:S(2)}, u32[]{:S(2)}) collective-permute-start(f32[3,4,64,256]{3,2,1,0:T(8,128)} %fusion.306), channel_id=1, source_target_pairs={{0,16},{16,32},{32,48},{48,64},{64,80},{80,96},{96,112},{112,128},... | collective-permute-start | bytes 2359304 | tf_op jit(solution)/shard_map/while/body/eval_jaxpr/ppermute | solution.py:32
  463.0 21.1 %collective-permute-start.4 = (f32[3,4,64,256]{3,2,1,0:T(8,128)}, f32[3,4,64,256]{3,2,1,0:T(8,128)S(1)}, u32[]{:S(2)}, u32[]{:S(2)}) collective-permute-start(f32[3,4,64,256]{3,2,1,0:T(8,128)} %fusion.306), channel_id=1, source_target_pairs={{0,16},{16,32},{32,48},{48,64},{64,80},{80,96},{96,112},{112,128},... | collective-permute-start | bytes 2359304 | tf_op jit(solution)/shard_map/while/body/eval_jaxpr/ppermute | solution.py:32
  720.1 26.5 %collective-permute-start.4 = (f32[3,4,64,256]{3,2,1,0:T(8,128)}, f32[3,4,64,256]{3,2,1,0:T(8,128)S(1)}, u32[]{:S(2)}, u32[]{:S(2)}) collective-permute-start(f32[3,4,64,256]{3,2,1,0:T(8,128)} %fusion.306), channel_id=1, source_target_pairs={{0,16},{16,32},{32,48},{48,64},{64,80},{80,96},{96,112},{112,128},... | collective-permute-start | bytes 2359304 | tf_op jit(solution)/shard_map/while/body/eval_jaxpr/ppermute | solution.py:32
  778.4 24.5 %collective-permute-start.4 = (f32[3,4,64,256]{3,2,1,0:T(8,128)}, f32[3,4,64,256]{3,2,1,0:T(8,128)S(1)}, u32[]{:S(2)}, u32[]{:S(2)}) collective-permute-start(f32[3,4,64,256]{3,2,1,0:T(8,128)} %fusion.306), channel_id=1, source_target_pairs={{0,16},{16,32},{32,48},{48,64},{64,80},{80,96},{96,112},{112,128},... | collective-permute-start | bytes 2359304 | tf_op jit(solution)/shard_map/while/body/eval_jaxpr/ppermute | solution.py:32
  810.7 22.2 %collective-permute-start.7 = (f32[3,4,66,1]{3,2,1,0:T(8,128)S(1)}, f32[3,4,66,1]{3,2,1,0:T(8,128)S(1)}, u32[]{:S(2)}, u32[]{:S(2)}) collective-permute-start(f32[3,4,66,1]{3,2,1,0:T(8,128)S(1)} %get-tuple-element.186), channel_id=1, source_target_pairs={{1,0},{0,1},{3,2},{2,3},{5,4},{4,5},{7,6},{6,7},{9,8},{8,9},{11,10... | collective-permute-start | bytes 9512 | tf_op jit(solution)/shard_map/ppermute | solution.py:22
  840.9 21.7 %collective-permute-start.11 = (f32[3,4,66,1]{3,2,1,0:T(8,128)S(1)}, f32[3,4,66,1]{3,2,1,0:T(8,128)S(1)}, u32[]{:S(2)}, u32[]{:S(2)}) collective-permute-start(f32[3,4,66,1]{3,2,1,0:T(8,128)S(1)} %get-tuple-element.184), channel_id=1, source_target_pairs={{1,0},{0,1},{3,2},{2,3},{5,4},{4,5},{7,6},{6,7},{9,8},{8,9},{11,10... | collective-permute-start | bytes 9512 | tf_op jit(solution)/shard_map/ppermute | solution.py:22
  865.2 46.8 %collective-permute-start.13 = (f32[3,4,64,256]{3,2,1,0:T(8,128)S(1)}, f32[3,4,64,256]{3,2,1,0:T(8,128)S(1)}, u32[]{:S(2)}, u32[]{:S(2)}) collective-permute-start(f32[3,4,64,256]{3,2,1,0:T(8,128)S(1)} %multiply_add_fusion.4), channel_id=1, source_target_pairs={{0,16},{16,32},{32,48},{48,64},{64,80},{80,96},{96,112},{112,128},... | collective-permute-start | bytes 2359304 | tf_op jit(solution)/shard_map/ppermute | solution.py:32
  871.8 29.4 %collective-permute-start.21 = (f32[3,4,66,1]{3,2,1,0:T(8,128)S(1)}, f32[3,4,66,1]{3,2,1,0:T(8,128)S(1)}, u32[]{:S(2)}, u32[]{:S(2)}) collective-permute-start(f32[3,4,66,1]{3,2,1,0:T(8,128)S(1)} %get-tuple-element.181), channel_id=1, source_target_pairs={{0,1},{1,0},{2,3},{3,2},{4,5},{5,4},{6,7},{7,6},{8,9},{9,8},{10,11... | collective-permute-start | bytes 9512 | tf_op jit(solution)/shard_map/ppermute | solution.py:20
  872.7 37.9 %collective-permute-start.20 = (f32[3,4,66,1]{3,2,1,0:T(8,128)S(1)}, f32[3,4,66,1]{3,2,1,0:T(8,128)S(1)}, u32[]{:S(2)}, u32[]{:S(2)}) collective-permute-start(f32[3,4,66,1]{3,2,1,0:T(8,128)S(1)} %get-tuple-element.182), channel_id=1, source_target_pairs={{1,0},{0,1},{3,2},{2,3},{5,4},{4,5},{7,6},{6,7},{9,8},{8,9},{11,10... | collective-permute-start | bytes 9512 | tf_op jit(solution)/shard_map/ppermute | solution.py:22
  948.9 21.2 %collective-permute-start.24 = (f32[3,4,66,1]{3,2,1,0:T(8,128)S(1)}, f32[3,4,66,1]{3,2,1,0:T(8,128)S(1)}, u32[]{:S(2)}, u32[]{:S(2)}) collective-permute-start(f32[3,4,66,1]{3,2,1,0:T(8,128)S(1)} %get-tuple-element.178), channel_id=1, source_target_pairs={{1,0},{0,1},{3,2},{2,3},{5,4},{4,5},{7,6},{6,7},{9,8},{8,9},{11,10... | collective-permute-start | bytes 9512 | tf_op jit(solution)/shard_map/ppermute | solution.py:22
  972.8 43.3 %collective-permute-start.26 = (f32[3,4,64,256]{3,2,1,0:T(8,128)S(1)}, f32[3,4,64,256]{3,2,1,0:T(8,128)S(1)}, u32[]{:S(2)}, u32[]{:S(2)}) collective-permute-start(f32[3,4,64,256]{3,2,1,0:T(8,128)S(1)} %multiply_add_fusion.2), channel_id=1, source_target_pairs={{0,16},{16,32},{32,48},{48,64},{64,80},{80,96},{96,112},{112,128},... | collective-permute-start | bytes 2359304 | tf_op jit(solution)/shard_map/ppermute | solution.py:32
  979.4 25.8 %collective-permute-start.34 = (f32[3,4,66,1]{3,2,1,0:T(8,128)S(1)}, f32[3,4,66,1]{3,2,1,0:T(8,128)S(1)}, u32[]{:S(2)}, u32[]{:S(2)}) collective-permute-start(f32[3,4,66,1]{3,2,1,0:T(8,128)S(1)} %get-tuple-element.175), channel_id=1, source_target_pairs={{0,1},{1,0},{2,3},{3,2},{4,5},{5,4},{6,7},{7,6},{8,9},{9,8},{10,11... | collective-permute-start | bytes 9512 | tf_op jit(solution)/shard_map/ppermute | solution.py:20
  980.8 33.8 %collective-permute-start.33 = (f32[3,4,66,1]{3,2,1,0:T(8,128)S(1)}, f32[3,4,66,1]{3,2,1,0:T(8,128)S(1)}, u32[]{:S(2)}, u32[]{:S(2)}) collective-permute-start(f32[3,4,66,1]{3,2,1,0:T(8,128)S(1)} %get-tuple-element.176), channel_id=1, source_target_pairs={{1,0},{0,1},{3,2},{2,3},{5,4},{4,5},{7,6},{6,7},{9,8},{8,9},{11,10... | collective-permute-start | bytes 9512 | tf_op jit(solution)/shard_map/ppermute | solution.py:22
  1021.0 22.6 %collective-permute-start.29 = (f32[3,4,66,1]{3,2,1,0:T(8,128)S(1)}, f32[3,4,66,1]{3,2,1,0:T(8,128)S(1)}, u32[]{:S(2)}, u32[]{:S(2)}) collective-permute-start(f32[3,4,66,1]{3,2,1,0:T(8,128)S(1)} %get-tuple-element.174), channel_id=1, source_target_pairs={{1,0},{0,1},{3,2},{2,3},{5,4},{4,5},{7,6},{6,7},{9,8},{8,9},{11,10... | collective-permute-start | bytes 9512 | tf_op jit(solution)/shard_map/ppermute | solution.py:22
  1051.6 22.6 %collective-permute-start.37 = (f32[3,4,66,1]{3,2,1,0:T(8,128)S(1)}, f32[3,4,66,1]{3,2,1,0:T(8,128)S(1)}, u32[]{:S(2)}, u32[]{:S(2)}) collective-permute-start(f32[3,4,66,1]{3,2,1,0:T(8,128)S(1)} %get-tuple-element.172), channel_id=1, source_target_pairs={{1,0},{0,1},{3,2},{2,3},{5,4},{4,5},{7,6},{6,7},{9,8},{8,9},{11,10... | collective-permute-start | bytes 9512 | tf_op jit(solution)/shard_map/ppermute | solution.py:22
  1077.3 44.5 %collective-permute-start.39 = (f32[3,4,64,256]{3,2,1,0:T(8,128)S(1)}, f32[3,4,64,256]{3,2,1,0:T(8,128)S(1)}, u32[]{:S(2)}, u32[]{:S(2)}) collective-permute-start(f32[3,4,64,256]{3,2,1,0:T(8,128)S(1)} %multiply_add_fusion), channel_id=1, source_target_pairs={{0,16},{16,32},{32,48},{48,64},{64,80},{80,96},{96,112},{112,128},... | collective-permute-start | bytes 2359304 | tf_op jit(solution)/shard_map/ppermute | solution.py:32
  1083.9 27.1 %collective-permute-start.47 = (f32[3,4,66,1]{3,2,1,0:T(8,128)S(1)}, f32[3,4,66,1]{3,2,1,0:T(8,128)S(1)}, u32[]{:S(2)}, u32[]{:S(2)}) collective-permute-start(f32[3,4,66,1]{3,2,1,0:T(8,128)S(1)} %get-tuple-element.167), channel_id=1, source_target_pairs={{0,1},{1,0},{2,3},{3,2},{4,5},{5,4},{6,7},{7,6},{8,9},{9,8},{10,11... | collective-permute-start | bytes 9512 | tf_op jit(solution)/shard_map/ppermute | solution.py:20
  1084.0 36.4 %collective-permute-start.46 = (f32[3,4,66,1]{3,2,1,0:T(8,128)S(1)}, f32[3,4,66,1]{3,2,1,0:T(8,128)S(1)}, u32[]{:S(2)}, u32[]{:S(2)}) collective-permute-start(f32[3,4,66,1]{3,2,1,0:T(8,128)S(1)} %get-tuple-element.168), channel_id=1, source_target_pairs={{1,0},{0,1},{3,2},{2,3},{5,4},{4,5},{7,6},{6,7},{9,8},{8,9},{11,10... | collective-permute-start | bytes 9512 | tf_op jit(solution)/shard_map/ppermute | solution.py:22
  1126.8 22.5 %collective-permute-start.42 = (f32[3,4,66,1]{3,2,1,0:T(8,128)S(1)}, f32[3,4,66,1]{3,2,1,0:T(8,128)S(1)}, u32[]{:S(2)}, u32[]{:S(2)}) collective-permute-start(f32[3,4,66,1]{3,2,1,0:T(8,128)S(1)} %get-tuple-element.170), channel_id=1, source_target_pairs={{1,0},{0,1},{3,2},{2,3},{5,4},{4,5},{7,6},{6,7},{9,8},{8,9},{11,10... | collective-permute-start | bytes 9512 | tf_op jit(solution)/shard_map/ppermute | solution.py:22
  1157.5 22.5 %collective-permute-start.50 = (f32[3,4,66,1]{3,2,1,0:T(8,128)S(1)}, f32[3,4,66,1]{3,2,1,0:T(8,128)S(1)}, u32[]{:S(2)}, u32[]{:S(2)}) collective-permute-start(f32[3,4,66,1]{3,2,1,0:T(8,128)S(1)} %get-tuple-element.166), channel_id=1, source_target_pairs={{1,0},{0,1},{3,2},{2,3},{5,4},{4,5},{7,6},{6,7},{9,8},{8,9},{11,10... | collective-permute-start | bytes 9512 | tf_op jit(solution)/shard_map/ppermute | solution.py:22
  (118 other events, 1082.0 us)
where the time goes:
time: 1190 us; the launch traced here: 1180 us
  waiting for transfers between devices  848 us (71%)
  starting transfers between devices  203 us (17%)
  other arithmetic  105 us (9%)
  local copies, waits for them, and re-layouts  24.6 us (2%)
    ppermute x52, waiting for transfers between devices, padded_2(): lax.ppermute(head, axis, [((i + 1) % count, i) for i in range(count)])  304 us
    ppermute x18, waiting for transfers between devices, passed_along(): lax.ppermute(value, axis, [(source, source + steps) for source in range(i...  282 us
    ppermute x52, waiting for transfers between devices, padded_2(): lax.ppermute(tail, axis, [(i, (i + 1) % count) for i in range(count)])  262 us
    ppermute x52, starting transfers between devices, padded_2(): lax.ppermute(tail, axis, [(i, (i + 1) % count) for i in range(count)])  107 us
    ppermute x52, starting transfers between devices, padded_2(): lax.ppermute(head, axis, [((i + 1) % count, i) for i in range(count)])  58.2 us
    ppermute x18, starting transfers between devices, passed_along(): lax.ppermute(value, axis, [(source, source + steps) for source in range(i...  38.2 us
  transfers between devices with their start and end apart: 122, of which 104 were waited for; matrix products, arithmetic and copies ran while one was open for 1% of the time, Pallas kernels for 0%

commit v1 on v0

v1 whole, which is shorter than its diff:
```python
import jax
import jax.numpy as jnp
from jax import lax
from jax.experimental import pallas as pl
from jax.experimental.pallas import tpu as pltpu
from jax.sharding import PartitionSpec as P

ITERS = 4
HALO = 23
STEP = 0.05
DEPTH = 8
TOP = 32
ROWS = 128
SHIFT = 87


def halo_rows(halo, body):
    first = (TOP - halo) // 8
    last = (TOP + 64 + halo + 7) // 8

    def run(block, carry):
        body(pl.multiple_of(block * 8, 8))
        return carry

    lax.fori_loop(first, last, run, 0)


def rates(field, coeffs, row, part):
    exchange_ref, slope_ref, axis_ref, demag_ref = coeffs
    rows = pl.ds(row, 8)
    above = pl.ds(row - 1, 8)
    below = pl.ds(row + 1, 8)
    cells = [[field[c, z, part, rows, :] for z in range(4)] for c in range(3)]
    out = []
    for z in range(4):
        sums = []
        slope_x = [None] * 3
        slope_y = [None] * 3
        for c in range(3):
            center = cells[c][z]
            x_next = field[c, z, part, below, :]
            x_prev = field[c, z, part, above, :]
            y_next = pltpu.roll(center, 127, 1)
            y_prev = pltpu.roll(center, 1, 1)
            z_pair = cells[c][min(z + 1, 3)] + cells[c][max(z - 1, 0)]
            sums.append((x_next + x_prev) + (y_next + y_prev) + z_pair)
            if c != 1:
                slope_x[c] = x_next - x_prev
            if c != 0:
                slope_y[c] = y_next - y_prev
        mx, my, mz = (cells[c][z] for c in range(3))
        exchange = exchange_ref[z, part, rows, :]
        slope = slope_ref[z, part, rows, :]
        axis = axis_ref[z, part, rows, :]
        hx = exchange * (sums[0] - 6.0 * mx) + slope * slope_x[2] + demag_ref[0, z, part, rows, :]
        hy = exchange * (sums[1] - 6.0 * my) + slope * slope_y[2] + demag_ref[1, z, part, rows, :]
        hz = exchange * sums[2] + axis * mz - slope * (slope_x[0] + slope_y[1]) + demag_ref[2, z, part, rows, :]
        ax, ay, az = 0.5 * mx, 0.5 * my, 0.5 * mz
        gx = hx + (ay * hz - az * hy)
        gy = hy + (az * hx - ax * hz)
        gz = hz + (ax * hy - ay * hx)
        out.append((gy * mz - gz * my, gz * mx - gx * mz, gx * my - gy * mx))
    return out, cells


def compute_kernel(index_ref, start_hbm, demag_ref, exchange_ref, slope_ref, axis_ref, end_ref, guess_ref,
                   state, node_one, extra, rate_zero, rate_one, rate_two, node_two, sem):
    me = index_ref[0]
    coeffs = (exchange_ref, slope_ref, axis_ref, demag_ref)
    copy = pltpu.make_async_copy(start_hbm, state.at[0], sem)
    copy.start()
    copy.wait()

    def put(ref, lead, z, part, row, values):
        for c in range(3):
            ref[(*lead, c, z, part, pl.ds(row, 8), slice(None))] = values[c]

    def get(ref, lead, z, part, row):
        return [ref[(*lead, c, z, part, pl.ds(row, 8), slice(None))] for c in range(3)]

    def assemble(field, out_ref):
        lane = lax.broadcasted_iota(jnp.int32, (8, 128), 1)

        def body(block, carry):
            row = pl.multiple_of(block * 8, 8)
            for c in range(3):
                for z in range(4):
                    a, b, d = (field[c, z, part, pl.ds(row + TOP, 8), :] for part in range(3))
                    out_ref[c, z, pl.ds(row, 8), 0:128] = jnp.where(lane < 84, pltpu.roll(a, 128 - 23, 1), pltpu.roll(b, 64, 1))
                    out_ref[c, z, pl.ds(row, 8), 128:256] = jnp.where(lane < 43, pltpu.roll(b, 64, 1), pltpu.roll(d, 23, 1))
            return carry

        lax.fori_loop(0, 8, body, 0)

    def slot_of(step):
        return jnp.where(step == 0, 0, 1 + lax.rem(step + 1, 2))

    def advance(step, carry):
        source = state.at[slot_of(step)]
        target = state.at[slot_of(step + 1)]
        halo = me - step + DEPTH - 1

        @pl.when(step < me - 3)
        def _():
            def body(row):
                for part in range(3):
                    out, cells = rates(source, coeffs, row, part)
                    for z in range(4):
                        put(target, (), z, part, row, [cells[c][z] + out[z][c] for c in range(3)])

            halo_rows(halo, body)

        @pl.when(step >= me - 3)
        def _():
            kept = step - me + 3

            def body(row):
                for part in range(3):
                    out, cells = rates(source, coeffs, row, part)
                    for z in range(4):
                        put(target, (), z, part, row, [cells[c][z] + out[z][c] for c in range(3)])
                        put(rate_zero, (kept,), z, part, row, out[z])
                        put(node_one, (kept,), z, part, row, [cells[c][z] + 0.5 * out[z][c] for c in range(3)])

            halo_rows(halo, body)

        @pl.when((step == 7) & (me > 12))
        def _():
            lane = lax.broadcasted_iota(jnp.int32, (8, 128), 1)

            def body(row):
                for c in range(3):
                    for z in range(4):
                        a, b, d = (target[c, z, part, pl.ds(row, 8), :] for part in range(3))
                        target[c, z, 0, pl.ds(row, 8), :] = jnp.where(lane < 107, a, pltpu.roll(b, SHIFT, 1))
                        target[c, z, 1, pl.ds(row, 8), :] = jnp.where(
                            lane < 20, pltpu.roll(a, 128 - SHIFT, 1), jnp.where(lane < 107, b, pltpu.roll(d, SHIFT, 1)))
                        target[c, z, 2, pl.ds(row, 8), :] = jnp.where(lane < 20, pltpu.roll(b, 128 - SHIFT, 1), d)

            halo_rows(halo, body)

        return carry

    lax.fori_loop(0, me + 1, advance, 0)
    assemble(state.at[slot_of(me)], guess_ref)

    for sweep in range(ITERS):
        halo = DEPTH - 2 - 2 * sweep

        def one_slice(count, carry, sweep=sweep, halo=halo):
            kept = 3 - count
            exists = me - count >= 0

            @pl.when(exists)
            def _():
                def body(row):
                    for part in range(3):
                        out, cells = rates(node_one.at[kept], coeffs, row, part)
                        for z in range(4):
                            new = [cells[c][z] + 0.5 * out[z][c] for c in range(3)]
                            if sweep:
                                add = get(extra, (kept,), z, part, row)
                                new = [new[c] + add[c] for c in range(3)]
                            put(node_two, (), z, part, row, new)
                            if sweep + 1 < ITERS:
                                put(rate_one, (kept,), z, part, row, out[z])

                halo_rows(halo, body)

            if sweep + 1 == ITERS:
                return carry

            @pl.when(jnp.logical_not(exists))
            def _():
                def body(row):
                    for part in range(3):
                        for z in range(4):
                            put(node_two, (), z, part, row, get(state, (0,), z, part, row))

                halo_rows(halo, body)

            @pl.when(count == 0)
            def _():
                def body(row):
                    for part in range(3):
                        out, cells = rates(node_two, coeffs, row, part)
                        for z in range(4):
                            put(rate_two, (), z, part, row, out[z])

                halo_rows(halo - 1, body)

            @pl.when(count > 0)
            def _():
                def body(row):
                    for part in range(3):
                        out, cells = rates(node_two, coeffs, row, part)
                        for z in range(4):
                            old = get(rate_zero, (kept + 1,), z, part, row)
                            mid = get(rate_one, (kept + 1,), z, part, row)
                            far = get(rate_two, (), z, part, row)
                            put(node_one, (kept + 1,), z, part, row, [
                                cells[c][z] + 0.5 * out[z][c] + (1.0 / 24.0) * (8.0 * mid[c] - 7.0 * old[c] - far[c])
                                for c in range(3)])
                            put(extra, (kept + 1,), z, part, row, [
                                (1.0 / 24.0) * ((far[c] - old[c]) + 4.0 * (far[c] - mid[c]))
                                for c in range(3)])
                            put(rate_zero, (kept + 1,), z, part, row, out[z])
                            put(rate_two, (), z, part, row, out[z])

                halo_rows(halo - 1, body)

            return carry

        lax.fori_loop(0, ITERS - sweep, one_slice, 0)
    assemble(node_two, end_ref)


def compute(index, start, demag, exchange, slope, axis, interpret=False):
    field = (3, 4, 3, ROWS, 128)
    vmem = pl.BlockSpec(memory_space=pltpu.VMEM)
    return pl.pallas_call(
        compute_kernel,
        name="llg",
        out_shape=[jax.ShapeDtypeStruct((3, 4, 64, 256), jnp.float32)] * 2,
        in_specs=[pl.BlockSpec(memory_space=pltpu.SMEM), pl.BlockSpec(memory_space=pl.ANY)] + [vmem] * 4,
        out_specs=[vmem] * 2,
        scratch_shapes=[
            pltpu.VMEM((3,) + field, jnp.float32),
            pltpu.VMEM((4,) + field, jnp.float32),
            pltpu.VMEM((4,) + field, jnp.float32),
            pltpu.VMEM((4,) + field, jnp.float32),
            pltpu.VMEM((4,) + field, jnp.float32),
            pltpu.VMEM(field, jnp.float32),
            pltpu.VMEM(field, jnp.float32),
            pltpu.SemaphoreType.DMA,
        ],
        compiler_params=pltpu.CompilerParams(vmem_limit_bytes=63 * 1024 * 1024),
        interpret=interpret,
    )(index, start, demag, exchange, slope, axis)


def blocked(padded):
    parts = jnp.stack([padded[..., SHIFT * k:SHIFT * k + 128] for k in range(3)], axis=2)
    edge = TOP - HALO
    return jnp.pad(parts, ((0, 0), (0, 0), (0, 0), (edge, ROWS - edge - padded.shape[2]), (0, 0)))


def coefficients(padded_region, material_table):
    columns = []
    for column in range(3):
        total = jnp.zeros(padded_region.shape, jnp.float32)
        for klass in range(material_table.shape[0]):
            total = total + (padded_region == klass).astype(jnp.float32) * material_table[klass, column]
        columns.append(total)
    exchange = STEP * columns[0]
    return exchange, (0.5 * STEP) * columns[1], (2.0 * STEP) * columns[2] - 6.0 * exchange


def from_padded(index, padded, material_table, interpret=False):
    fields = blocked(padded)
    exchange, slope, axis = coefficients(fields[6], material_table)
    return compute(index, fields[:3], fields[3:6], exchange, slope, axis, interpret)


def on_device(start_field, demag_field, region_map, material_table):
    tile = jnp.concatenate([start_field, STEP * demag_field, region_map.astype(jnp.float32)[None]], axis=0)
    strips = jnp.concatenate([tile[..., :HALO], tile[..., -HALO:]], axis=3)
    pairs = [(2 * t + g, 2 * (t ^ 1) + (g ^ 1)) for t in range(16) for g in range(2)]
    strips = lax.ppermute(strips, ("tm", "gy"), pairs)
    tile = jnp.concatenate([strips[..., HALO:], tile, strips[..., :HALO]], axis=3)
    count = lax.axis_size("gx")
    above = lax.ppermute(tile[:, :, -HALO:], "gx", [(i, (i + 1) % count) for i in range(count)])
    below = lax.ppermute(tile[:, :, :HALO], "gx", [((i + 1) % count, i) for i in range(count)])
    padded = jnp.concatenate([above, tile, below], axis=2)
    index = lax.axis_index("tm").astype(jnp.int32)[None]
    end, guess = from_padded(index, padded, material_table)
    return end[None], guess[None]


def solution(mesh):
    placed = (P(None, None, "gx", "gy"), P(None, None, "gx", "gy"), P(None, "gx", "gy"), P())
    return jax.shard_map(
        on_device,
        mesh=mesh,
        in_specs=placed,
        out_specs=(P("tm", None, None, "gx", "gy"), P("tm", None, None, "gx", "gy")),
        check_vma=False,
    )
```

time: 1190 us -> 187 us (0.16)
  the two profiles are of different devices: /device:TPU:159 before, /device:TPU:230 now
where the time goes in v1:
time: 187 us; the launch traced here: 186 us
  Pallas kernels  117 us (63%)
  waiting for transfers between devices  30.4 us (16%)
  other arithmetic  23.4 us (13%)
  local copies, waits for them, and re-layouts  12.5 us (7%)
  starting transfers between devices  2.15 us (1%)
    pallas_call x1, Pallas kernels, compute(): pl.pallas_call(compute_kernel, name='llg', out_shape=[jax.ShapeDtypeStruc...  117 us
    ppermute x1, waiting for transfers between devices, on_device(): strips = lax.ppermute(strips, ('tm', 'gy'), pairs)  17.3 us
    ppermute x1, waiting for transfers between devices, on_device(): lax.ppermute(tile[:, :, :HALO], 'gx', [((i + 1) % count, i) for i in rang...  10.1 us
    mul x1, other arithmetic, coefficients(): 0.5 * STEP * columns[1]  6.87 us
    sub x1, other arithmetic, coefficients(): 2.0 * STEP * columns[2] - 6.0 * exchange  6.79 us
  transfers between devices with their start and end apart: 3, of which 3 were waited for; matrix products, arithmetic and copies ran while one was open for 2% of the time, Pallas kernels for 0%

profile of v1, /device:TPU:230, one launch (start us, length us, event | category | flops | bytes accessed | tf_op | source)
XLA Modules:
  0.0 186.0 jit_solution(9778379072430531358)
XLA Ops:
  0.6 1.0 convert_bitcast_fusion
  1.6 1.3 broadcast_multiply_fusion
  2.9 1.3 pad_maximum_fusion.1
  4.9 0.4 copy.8
  5.3 0.6 collective-permute-start
  5.8 17.3 %collective-permute-done = f32[7,4,64,46]{2,1,3,0:T(4,128)S(1)} collective-permute-done((f32[7,4,64,46]{2,1,3,0:T(4,128)S(1)}, f32[7,4,64,46]{2,1,3,0:T(4,128)S(1)}, u32[]{:S(2)}, u32[]{:S(2)}) %collective-permute-start) | collective-permute-done | bytes 329760 | tf_op jit(solution)/shard_map/ppermute | solution.py:269
  23.1 0.8 fusion.3
  24.2 1.3 copy.18
  25.6 1.7 pad_maximum_fusion.6
  27.3 1.2 copy.12
  28.5 1.6 collective-permute-start.2
  30.1 1.2 copy.11
  31.3 0.7 fusion.4
  32.0 10.1 %collective-permute-done.2 = f32[7,4,23,302]{3,1,2,0:T(4,128)} collective-permute-done((f32[7,4,23,302]{3,1,2,0:T(4,128)}, f32[7,4,23,302]{3,1,2,0:T(4,128)}, u32[]{:S(2)}, u32[]{:S(2)}) %collective-permute-start.2) | collective-permute-done | bytes 777984 | tf_op jit(solution)/shard_map/ppermute | solution.py:273
  42.1 1.3 copy.14
  43.4 3.0 %collective-permute-done.1 = f32[7,4,23,302]{3,1,2,0:T(4,128)} collective-permute-done((f32[7,4,23,302]{3,1,2,0:T(4,128)}, f32[7,4,23,302]{3,1,2,0:T(4,128)}, u32[]{:S(2)}, u32[]{:S(2)}) %collective-permute-start.1) | collective-permute-done | bytes 777984 | tf_op jit(solution)/shard_map/ppermute | solution.py:272
  46.5 1.3 copy.13
  47.7 3.3 %pad_maximum_fusion = f32[7,4,110,302]{3,2,1,0:T(8,128)S(1)} fusion(f32[7,4,23,302]{3,2,1,0:T(8,128)S(1)} %copy.14, f32[7,4,64,23]{3,2,1,0:T(8,128)S(1)} %copy.18, f32[1,4,64,256]{3,2,1,0:T(8,128)} %copy-done.1, f32[3,4,64,256]{3,2,1,0:T(8,128)S(1)} %broadcast_multiply_fusion, f32[3,4,64,256]{3,2,1,0:T(8,128)S(1)} %copy-done, f32[7,4,64,23]{3,2,1,0:T(8,128)S(1)} %copy.17, ...), kind=kLoop, calls=%fused_computation.5 | loop fusion | flops 5580960 | bytes 7441280 | tf_op jit(solution)/shard_map/concatenate | solution.py:274
  51.0 0.9 slice_bitcast_fusion.2
  52.0 0.9 select_maximum_fusion
  52.8 2.7 %fusion.1 = (f32[3,4,3,128,128]{4,3,2,1,0:T(8,128)}, f32[3,4,3,128,128]{4,3,2,1,0:T(8,128)}) fusion(f32[7,4,3,128,128]{4,3,2,1,0:T(8,128)S(1)} %select_maximum_fusion), kind=kLoop, calls=%fused_computation.26 | loop fusion | bytes 9437184 | tf_op jit(solution)/shard_map/slice | solution.py:262
  55.5 6.8 %subtract_bitcast_fusion = (f32[4,3,128,128]{3,2,1,0:T(8,128)}, pred[1,4,3,128,128]{4,3,2,1,0:T(8,128)(4,1)S(1)}, pred[1,4,3,128,128]{4,3,2,1,0:T(8,128)(4,1)S(1...) fusion(f32[]{:T(128)} %bitcast.20, f32[]{:T(128)} %bitcast.19, f32[]{:T(128)} %bitcast.18, ...), kind=kLoop, calls=%fused_computation.16 | loop fusion | flops 4128768 | bytes 2359328 | tf_op jit(solution)/shard_map/sub | solution.py:256
  62.3 6.9 %multiply_bitcast_fusion = (f32[4,3,128,128]{3,2,1,0:T(8,128)}, f32[4,3,128,128]{3,2,1,0:T(8,128)}) fusion(pred[1,4,3,128,128]{4,3,2,1,0:T(8,128)(4,1)S(1)} %get-tuple-element.10, pred[1,4,3,128,128]{4,3,2,1,0:T(8,128)(4,1)S(1)} %get-tuple-element.9, pred[1,4,3,128,128]{4,3,2,1,0:T(8,128)(4,1)S(1)} %get-tuple-element.8, ...), kind=kLoop, calls=%fused_computation.17 | loop fusion | flops 3145728 | bytes 2359328 | tf_op jit(solution)/shard_map/mul | solution.py:256
  69.2 116.8 %llg.1 = (f32[3,4,64,256]{3,2,1,0:T(8,128)}, f32[3,4,64,256]{3,2,1,0:T(8,128)}) custom-call(s32[1]{0:T(128)} %bitcast.index_ref, f32[3,4,3,128,128]{4,3,2,1,0:T(8,128)} %get-tuple-element.12.start_hbm, f32[3,4,3,128,128]{4,3,2,1,0:T(8,128)} %get-tuple-element.11.demag_ref, f32[4,3,128,128]{3,2,1,0:T(8,128)} %get-tuple-element.21.exchange_ref, ...), custom_call_target="tpu_custom_call" | custom-call | tf_op jit(solution)/shard_map/llg/pallas_call | solution.py:221
  (10 shorter events, 1.0 us)
Async XLA Ops:
  1.6 2.9 %copy-start.1 = (f32[1,4,64,256]{3,2,1,0:T(8,128)}, f32[1,4,64,256]{3,2,1,0:T(8,128)S(1)}, u32[]{:S(2)}) copy-start(f32[1,4,64,256]{3,2,1,0:T(8,128)S(1)} %convert_bitcast_fusion) | copy-start | bytes 786436
  4.5 21.0 %copy-start = (f32[3,4,64,256]{3,2,1,0:T(8,128)S(1)}, f32[3,4,64,256]{3,2,1,0:T(8,128)}, u32[]{:S(2)}) copy-start(f32[3,4,64,256]{3,2,1,0:T(8,128)} %param.4) | copy-start | bytes 2359300
  5.3 17.9 %collective-permute-start = (f32[7,4,64,46]{2,1,3,0:T(4,128)S(1)}, f32[7,4,64,46]{2,1,3,0:T(4,128)S(1)}, u32[]{:S(2)}, u32[]{:S(2)}) collective-permute-start(f32[7,4,64,46]{2,1,3,0:T(4,128)S(1)} %copy.8), channel_id=1, source_target_pairs={{0,17},{1,16},{16,1},{17,0},{32,49},{33,48},{48,33},{49,32},{64,81... | collective-permute-start | bytes 989192 | tf_op jit(solution)/shard_map/ppermute | solution.py:269
  25.6 5.8 %copy-start.2 = (f32[4,3]{1,0:T(4,128)S(1)}, f32[4,3]{1,0:T(4,128)}, u32[]{:S(2)}) copy-start(f32[4,3]{1,0:T(4,128)} %param.7) | copy-start | bytes 148
  28.5 13.6 %collective-permute-start.2 = (f32[7,4,23,302]{3,1,2,0:T(4,128)}, f32[7,4,23,302]{3,1,2,0:T(4,128)}, u32[]{:S(2)}, u32[]{:S(2)}) collective-permute-start(f32[7,4,23,302]{3,1,2,0:T(4,128)} %copy.12), channel_id=1, source_target_pairs={{2,0},{4,2},{6,4},{8,6},{10,8},{12,10},{14,12},{0,14},{3,1},{5,3},... | collective-permute-start | bytes 2333864 | tf_op jit(solution)/shard_map/ppermute | solution.py:273
  31.3 15.1 %collective-permute-start.1 = (f32[7,4,23,302]{3,1,2,0:T(4,128)}, f32[7,4,23,302]{3,1,2,0:T(4,128)}, u32[]{:S(2)}, u32[]{:S(2)}) collective-permute-start(f32[7,4,23,302]{3,1,2,0:T(4,128)} %copy.11), channel_id=1, source_target_pairs={{0,2},{2,4},{4,6},{6,8},{8,10},{10,12},{12,14},{14,0},{1,3},{3,5},... | collective-permute-start | bytes 2333864 | tf_op jit(solution)/shard_map/ppermute | solution.py:272

commit v2 on v1

v2 whole, which is shorter than its diff:
```python
import jax
import jax.numpy as jnp
from jax import lax
from jax.experimental import pallas as pl
from jax.experimental.pallas import tpu as pltpu
from jax.sharding import PartitionSpec as P

MESH = pl.DeviceIdType.MESH
ITERS = 4
HALO = 24
SIDE = 32
STEP = 0.05
DEPTH = 8
FIRST = 8
LAST = 64
ROWS = 72
PARTS = 5


def blocks_of(halo):
    return (FIRST + HALO - halo) // 8, LAST // 8


def lanes():
    return lax.broadcasted_iota(jnp.int32, (8, 128), 1)


def prepare(field, sum_ref, difference_ref, row):
    rows = pl.ds(row, 8)
    lane = lanes()
    first, last = lane == 0, lane == 127
    for c in range(3):
        for z in range(4):
            v = [field[c, z, part, rows, :] for part in range(PARTS)]
            n = [pltpu.roll(x, 127, 1) for x in v]
            p = [pltpu.roll(x, 1, 1) for x in v]
            following = [
                jnp.where(last, n[1], n[0]),
                jnp.where(last, n[4], n[1]),
                jnp.where(last, n[3], n[2]),
                jnp.where(last, pltpu.roll(v[4], 95, 1), n[3]),
                jnp.where(last, n[0], jnp.where(lane == 95, pltpu.roll(v[2], 95, 1), n[4])),
            ]
            previous = [
                jnp.where(first, p[4], p[0]),
                jnp.where(first, p[0], p[1]),
                jnp.where(first, pltpu.roll(v[4], 33, 1), p[2]),
                jnp.where(first, p[2], p[3]),
                jnp.where(first, p[1], jnp.where(lane == 32, pltpu.roll(v[3], 33, 1), p[4])),
            ]
            for part in range(PARTS):
                sum_ref[c, z, part, rows, :] = following[part] + previous[part]
                if c:
                    difference_ref[c - 1, z, part, rows, :] = following[part] - previous[part]


def join_halves(field):
    lane = lax.broadcasted_iota(jnp.int32, (1, 128), 1)
    down = (lane < 32) | ((lane >= 64) & (lane < 96))
    edge, beyond = pl.ds(LAST - 1, 1), pl.ds(LAST, 1)
    for c in range(3):
        for z in range(4):
            for part in range(4):
                field[c, z, part, beyond, :] = field[c, z, (part + 2) % 4, edge, :]
            side = field[c, z, 4, edge, :]
            field[c, z, 4, beyond, :] = jnp.where(down, pltpu.roll(side, 96, 1), pltpu.roll(side, 32, 1))


def rates(field, aux, row, part):
    exchange_ref, slope_ref, signed_ref, axis_ref, demag_ref, sum_ref, difference_ref = aux
    rows = pl.ds(row, 8)
    above = pl.ds(row - 1, 8)
    below = pl.ds(row + 1, 8)
    cells = [[field[c, z, part, rows, :] for z in range(4)] for c in range(3)]
    out = []
    for z in range(4):
        sums = []
        slope_x = [None] * 3
        for c in range(3):
            x_next = field[c, z, part, below, :]
            x_prev = field[c, z, part, above, :]
            z_pair = cells[c][min(z + 1, 3)] + cells[c][max(z - 1, 0)]
            sums.append((x_next + x_prev) + sum_ref[c, z, part, rows, :] + z_pair)
            if c != 1:
                slope_x[c] = x_next - x_prev
        mx, my, mz = (cells[c][z] for c in range(3))
        exchange = exchange_ref[z, part, rows, :]
        slope = slope_ref[z, part, rows, :]
        signed = signed_ref[z, part, rows, :]
        axis = axis_ref[z, part, rows, :]
        hx = exchange * (sums[0] - 6.0 * mx) + signed * slope_x[2] + demag_ref[0, z, part, rows, :]
        hy = exchange * (sums[1] - 6.0 * my) + slope * difference_ref[1, z, part, rows, :] + demag_ref[1, z, part, rows, :]
        hz = (exchange * sums[2] + axis * mz
              - (signed * slope_x[0] + slope * difference_ref[0, z, part, rows, :]) + demag_ref[2, z, part, rows, :])
        ax, ay, az = 0.5 * mx, 0.5 * my, 0.5 * mz
        gx = hx + (ay * hz - az * hy)
        gy = hy + (az * hx - ax * hz)
        gz = hz + (ax * hy - ay * hx)
        out.append((gy * mz - gz * my, gz * mx - gx * mz, gx * my - gy * mx))
    return out, cells


def put(ref, lead, z, part, row, values):
    for c in range(3):
        ref[(*lead, c, z, part, pl.ds(row, 8), slice(None))] = values[c]


def get(ref, lead, z, part, row):
    return [ref[(*lead, c, z, part, pl.ds(row, 8), slice(None))] for c in range(3)]


def evaluate(field, aux, halo, use):
    first, last = blocks_of(halo)
    join_halves(field)
    prepare(field, aux[5], aux[6], pl.multiple_of(first * 8, 8))

    def run(block, carry):
        row = pl.multiple_of(block * 8, 8)
        prepare(field, aux[5], aux[6], row + 8)
        for part in range(PARTS):
            out, cells = rates(field, aux, row, part)
            use(row, part, out, cells)
        return carry

    lax.fori_loop(first, last, run, 0)


def assemble(field, out_ref):
    upside_down = 7 - lax.broadcasted_iota(jnp.int32, (8, 128), 0)

    def body(block, carry):
        row = pl.multiple_of(block * 8, 8)
        for c in range(3):
            for z in range(4):
                for part in range(2):
                    columns = slice(128 * part, 128 * part + 128)
                    out_ref[c, z, pl.ds(row, 8), columns] = field[c, z, part, pl.ds(FIRST + HALO + row, 8), :]
                    out_ref[c, z, pl.ds(row + 32, 8), columns] = jnp.take_along_axis(
                        field[c, z, part + 2, pl.ds(LAST - 8 - row, 8), :], upside_down, axis=0)
        return carry

    lax.fori_loop(0, 4, body, 0)


def fill_coefficients(table, region, exchange_ref, slope_ref, signed_ref, axis_ref):
    lane = lanes()
    upper_side = (lane < 32) | (lane >= 96)

    def body(block, carry):
        rows = pl.ds(pl.multiple_of(block * 8, 8), 8)
        for z in range(4):
            for part in range(PARTS):
                kind = region[z, part, rows, :]
                exchange, slope, axis = (
                    jnp.where(kind == 0.0, table[0, k], jnp.where(kind == 1.0, table[1, k], jnp.where(
                        kind == 2.0, table[2, k], table[3, k]))) for k in range(3))
                exchange = STEP * exchange
                slope = (0.5 * STEP) * slope
                exchange_ref[z, part, rows, :] = exchange
                slope_ref[z, part, rows, :] = slope
                signed_ref[z, part, rows, :] = (
                    slope if part < 2 else -slope if part < 4 else jnp.where(upper_side, slope, -slope))
                axis_ref[z, part, rows, :] = (2.0 * STEP) * axis - 6.0 * exchange
        return carry

    lax.fori_loop(FIRST // 8, LAST // 8, body, 0)


def compute_kernel(index_ref, table, fields, end_ref, guess_ref,
                   state_even, state_odd, node_one, extra, rate_zero, rate_one, rate_two, node_two, sum_ref, difference_ref,
                   demag_ref, region, exchange_ref, slope_ref, signed_ref, axis_ref, sems):
    me = index_ref[0]
    aux = (exchange_ref, slope_ref, signed_ref, axis_ref, demag_ref, sum_ref, difference_ref)
    loads = [
        pltpu.make_async_copy(fields.at[6], region, sems.at[0]),
        pltpu.make_async_copy(fields.at[0:3], state_even, sems.at[1]),
        pltpu.make_async_copy(fields.at[3:6], demag_ref, sems.at[2]),
    ]
    for copy in loads:
        copy.start()
    loads[0].wait()
    fill_coefficients(table, region, exchange_ref, slope_ref, signed_ref, axis_ref)
    loads[1].wait()
    loads[2].wait()

    def load_start(target):
        copy = pltpu.make_async_copy(fields.at[0:3], target, sems.at[3])
        copy.start()
        copy.wait()

    def step_from(source, target, step):
        halo = me - step + DEPTH - 1

        @pl.when(step < me - 3)
        def _():
            def use(row, part, out, cells):
                for z in range(4):
                    put(target, (), z, part, row, [cells[c][z] + out[z][c] for c in range(3)])

            evaluate(source, aux, halo, use)

        @pl.when(step >= me - 3)
        def _():
            kept = step - me + 3

            def use(row, part, out, cells):
                for z in range(4):
                    put(target, (), z, part, row, [cells[c][z] + out[z][c] for c in range(3)])
                    put(rate_zero, (kept,), z, part, row, out[z])
                    put(node_one, (kept,), z, part, row, [cells[c][z] + 0.5 * out[z][c] for c in range(3)])

            evaluate(source, aux, halo, use)

    def advance(step, carry):
        even = lax.rem(step, 2) == 0
        pl.when(even)(lambda: step_from(state_even, state_odd, step))
        pl.when(jnp.logical_not(even))(lambda: step_from(state_odd, state_even, step))
        return carry

    lax.fori_loop(0, me + 1, advance, 0)
    pl.when(lax.rem(me, 2) == 0)(lambda: assemble(state_even, guess_ref))
    pl.when(lax.rem(me, 2) == 1)(lambda: assemble(state_odd, guess_ref))

    def sweep_slices(sweep, carry):
        halo = DEPTH - 2 - 2 * sweep

        def one_slice(count, carry):
            kept = 3 - count

            @pl.when((me - count >= 0) & (sweep == 0))
            def _():
                def use(row, part, out, cells):
                    for z in range(4):
                        put(node_two, (), z, part, row, [cells[c][z] + 0.5 * out[z][c] for c in range(3)])
                        put(rate_one, (kept,), z, part, row, out[z])

                evaluate(node_one.at[kept], aux, halo, use)

            @pl.when((me - count >= 0) & (sweep > 0))
            def _():
                def use(row, part, out, cells):
                    for z in range(4):
                        add = get(extra, (kept - 1,), z, part, row)
                        put(node_two, (), z, part, row, [cells[c][z] + 0.5 * out[z][c] + add[c] for c in range(3)])
                        put(rate_one, (kept,), z, part, row, out[z])

                evaluate(node_one.at[kept], aux, halo, use)

            pl.when((me - count == -1) & (sweep + 1 < ITERS))(lambda: load_start(node_two))

            @pl.when((count == 0) & (sweep + 1 < ITERS))
            def _():
                def use(row, part, out, cells):
                    for z in range(4):
                        put(rate_two, (), z, part, row, out[z])

                evaluate(node_two, aux, halo - 1, use)

            @pl.when((count > 0) & (me - count >= -1) & (sweep + 1 < ITERS))
            def _():
                def use(row, part, out, cells):
                    for z in range(4):
                        old = get(rate_zero, (kept + 1,), z, part, row)
                        mid = get(rate_one, (kept + 1,), z, part, row)
                        far = get(rate_two, (), z, part, row)
                        put(node_one, (kept + 1,), z, part, row, [
                            cells[c][z] + 0.5 * out[z][c] + (1.0 / 24.0) * (8.0 * mid[c] - 7.0 * old[c] - far[c])
                            for c in range(3)])
                        put(extra, (kept,), z, part, row, [
                            (1.0 / 24.0) * ((far[c] - old[c]) + 4.0 * (far[c] - mid[c]))
                            for c in range(3)])
                        put(rate_zero, (kept + 1,), z, part, row, out[z])
                        put(rate_two, (), z, part, row, out[z])

                evaluate(node_two, aux, halo - 1, use)

            return carry

        return lax.fori_loop(0, ITERS - sweep, one_slice, carry)

    lax.fori_loop(0, ITERS, sweep_slices, 0)
    assemble(node_two, end_ref)


def compute(index, table, fields, interpret=False):
    field = (3, 4, PARTS, ROWS, 128)
    vmem = pl.BlockSpec(memory_space=pltpu.VMEM)
    smem = pl.BlockSpec(memory_space=pltpu.SMEM)
    return pl.pallas_call(
        compute_kernel,
        name="llg",
        out_shape=[jax.ShapeDtypeStruct((3, 4, 64, 256), jnp.float32)] * 2,
        in_specs=[smem, smem, pl.BlockSpec(memory_space=pl.ANY)],
        out_specs=[vmem] * 2,
        scratch_shapes=[
            pltpu.VMEM(field, jnp.float32),
            pltpu.VMEM(field, jnp.float32),
            pltpu.VMEM((4,) + field, jnp.float32),
            pltpu.VMEM((3,) + field, jnp.float32),
            pltpu.VMEM((4,) + field, jnp.float32),
            pltpu.VMEM((4,) + field, jnp.float32),
            pltpu.VMEM(field, jnp.float32),
            pltpu.VMEM(field, jnp.float32),
            pltpu.VMEM(field, jnp.float32),
            pltpu.VMEM((2,) + field[1:], jnp.float32),
            pltpu.VMEM(field, jnp.float32),
        ] + [pltpu.VMEM(field[1:], jnp.float32)] * 5 + [pltpu.SemaphoreType.DMA((4,))],
        compiler_params=pltpu.CompilerParams(vmem_limit_bytes=62 * 1024 * 1024),
        interpret=interpret,
    )(index, table, fields)


def halo_kernel(start_ref, demag_ref, region_ref, out_ref, own, down, up, side_out, side_in, corner_out, corner_in, corner,
                send_sems, recv_sems, local_sems):
    gx, gy, tm = lax.axis_index("gx"), lax.axis_index("gy"), lax.axis_index("tm")
    count = lax.axis_size("gx")
    after = {"gx": lax.rem(gx + 1, count)}
    before = {"gx": lax.rem(gx + count - 1, count)}
    across = {"tm": tm + 1 - 2 * lax.rem(tm, 2), "gy": 1 - gy}
    barrier = pltpu.get_barrier_semaphore()
    for device in (after, before, across):
        pl.semaphore_signal(barrier, inc=1, device_id=device, device_id_type=MESH)

    upside_down = 7 - lax.broadcasted_iota(jnp.int32, (8, 128), 0)
    lane = lanes()

    def flip(value):
        return jnp.take_along_axis(value, upside_down, axis=0)

    def load(f, z, row, part):
        at = (z, slice(row, row + 8), slice(128 * part, 128 * part + 128))
        if f < 3:
            return start_ref[(f,) + at]
        if f < 6:
            return STEP * demag_ref[(f - 3,) + at]
        return region_ref[at].astype(jnp.float32)

    def quarters(a, b, c, d):
        return jnp.where(lane < 64, jnp.where(lane < 32, a, b), jnp.where(lane < 96, c, d))

    def stage(z, carry):
        for f in range(7):
            for k in range(4):
                rows = slice(8 * k, 8 * k + 8)
                a = [load(f, z, 8 * k, part) for part in range(2)]
                b = [flip(load(f, z, 56 - 8 * k, part)) for part in range(2)]
                for part in range(2):
                    own[f, z, part, rows, :] = a[part]
                    own[f, z, part + 2, rows, :] = b[part]
                side_out[f, z, rows, :] = quarters(a[0], pltpu.roll(b[0], 32, 1), pltpu.roll(b[1], 96, 1), a[1])
            for k in range(3):
                rows = slice(8 * k, 8 * k + 8)
                for part in range(2):
                    down[f, z, part, rows, :] = load(f, z, 40 + 8 * k, part)
                    up[f, z, part, rows, :] = flip(load(f, z, 16 - 8 * k, part))
        return carry

    lax.fori_loop(0, 4, stage, 0)
    pl.semaphore_wait(barrier, 3)

    def send(number, source, target, device):
        copy = pltpu.make_async_remote_copy(source, target, send_sems.at[number], recv_sems.at[number],
                                            device_id=device, device_id_type=MESH)
        copy.start()
        return copy

    near, far = slice(0, HALO), slice(HALO, 32)
    sides = [send(k, side_out.at[:, :, rows, :], side_in.at[:, :, rows, :], across) for k, rows in enumerate((near, far))]
    edge, inner = slice(FIRST, FIRST + HALO), slice(FIRST + HALO, LAST)
    edges = [send(2, down, out_ref.at[:, :, 0:2, edge, :], after), send(3, up, out_ref.at[:, :, 2:4, edge, :], before)]
    middle = pltpu.make_async_copy(own, out_ref.at[:, :, 0:4, inner, :], local_sems.at[0])
    middle.start()
    sides[0].wait_recv()

    def turn(pair, carry):
        for f in range(7):
            for k in range(3):
                rows = slice(8 * k, 8 * k + 8)
                back = slice(16 - 8 * k, 24 - 8 * k)
                one = flip(side_in[f, pair, back, :])
                two = flip(side_in[f, pair + 2, back, :])
                one_left, one_right = pltpu.roll(one, 96, 1), pltpu.roll(one, 32, 1)
                two_left, two_right = pltpu.roll(two, 96, 1), pltpu.roll(two, 32, 1)
                corner_out[0, f, pair, rows, :] = quarters(one_left, two_left, two_right, one_right)
                corner_out[1, f, pair, rows, :] = quarters(two_right, one_right, one_left, two_left)
        return carry

    lax.fori_loop(0, 2, turn, 0)
    corners = [send(4, corner_out.at[0], corner_in.at[0], after), send(5, corner_out.at[1], corner_in.at[1], before)]
    sides[1].wait_recv()
    strip = pltpu.make_async_copy(side_in, out_ref.at[:, :, 4, inner, :], local_sems.at[1])
    strip.start()
    corners[0].wait_recv()
    corners[1].wait_recv()
    mid = (lane >= 32) & (lane < 96)

    def unpack(pair, carry):
        for f in range(7):
            for k in range(3):
                rows = slice(8 * k, 8 * k + 8)
                upper, lower = corner_in[0, f, pair, rows, :], corner_in[1, f, pair, rows, :]
                corner[f, pair, rows, :] = jnp.where(mid, lower, upper)
                corner[f, pair + 2, rows, :] = pltpu.roll(jnp.where(mid, upper, lower), 64, 1)
        return carry

    lax.fori_loop(0, 2, unpack, 0)
    last = pltpu.make_async_copy(corner, out_ref.at[:, :, 4, edge, :], local_sems.at[2])
    last.start()
    for copy in edges:
        copy.wait()
    for copy in sides + corners:
        copy.wait_send()
    middle.wait()
    strip.wait()
    last.wait()


def gather_halo(start_field, demag_field, region_map):
    vmem = pl.BlockSpec(memory_space=pltpu.VMEM)
    return pl.pallas_call(
        halo_kernel,
        name="halo",
        out_shape=jax.ShapeDtypeStruct((7, 4, PARTS, ROWS, 128), jnp.float32),
        in_specs=[vmem] * 3,
        out_specs=pl.BlockSpec(memory_space=pl.ANY),
        scratch_shapes=[
            pltpu.VMEM((7, 4, 4, 32, 128), jnp.float32),
            pltpu.VMEM((7, 4, 2, HALO, 128), jnp.float32),
            pltpu.VMEM((7, 4, 2, HALO, 128), jnp.float32),
            pltpu.VMEM((7, 4, 32, 128), jnp.float32),
            pltpu.VMEM((7, 4, 32, 128), jnp.float32),
            pltpu.VMEM((2, 7, 2, HALO, 128), jnp.float32),
            pltpu.VMEM((2, 7, 2, HALO, 128), jnp.float32),
            pltpu.VMEM((7, 4, HALO, 128), jnp.float32),
            pltpu.SemaphoreType.DMA((6,)),
            pltpu.SemaphoreType.DMA((6,)),
            pltpu.SemaphoreType.DMA((3,)),
        ],
        compiler_params=pltpu.CompilerParams(
            collective_id=0, has_side_effects=True, vmem_limit_bytes=40 * 1024 * 1024),
    )(start_field, demag_field, region_map)


def on_device(start_field, demag_field, region_map, material_table):
    fields = gather_halo(start_field, demag_field, region_map)
    index = lax.axis_index("tm").astype(jnp.int32)[None]
    end, guess = compute(index, material_table, fields)
    return end[None], guess[None]


def solution(mesh):
    placed = (P(None, None, "gx", "gy"), P(None, None, "gx", "gy"), P(None, "gx", "gy"), P())
    return jax.shard_map(
        on_device,
        mesh=mesh,
        in_specs=placed,
        out_specs=(P("tm", None, None, "gx", "gy"), P("tm", None, None, "gx", "gy")),
        check_vma=False,
    )
```

time: 187 us -> 104 us (0.56)
  waiting for transfers between devices: 30.4 us -> 0 us
  other arithmetic: 23.4 us -> 0 us
  Pallas kernels: 117 us -> 95.8 us
  local copies, waits for them, and re-layouts: 12.5 us -> 5.49 us
  starting transfers between devices: 2.15 us -> 0 us
    pallas_call x1, Pallas kernels: 117 us -> 79.4 us  [compute(): pl.pallas_call(compute_kernel, name='llg', out_shape=[jax.ShapeDtypeStruc...]
    ppermute x3 -> x0, waiting for transfers between devices: 30.4 us -> none  [the longest x1 17.3 us: on_device(): strips = lax.ppermute(strips, ('tm', 'gy'), pairs)]
    pallas_call x0 -> x1, Pallas kernels: none -> 16.4 us  [gather_halo(): pl.pallas_call(halo_kernel, name='halo', out_shape=jax.ShapeDtypeStruct((...]
    mul x2 -> x0, other arithmetic: 8.18 us -> none  [the longest x1 6.87 us: coefficients(): 0.5 * STEP * columns[1]]
    slice x6 -> x0, local copies, waits for them, and re-layouts: 6.91 us -> none  [the longest x1 2.7 us: from_padded(): fields[3:6]]
    sub x1 -> x0, other arithmetic: 6.79 us -> none  [coefficients(): 2.0 * STEP * columns[2] - 6.0 * exchange]
    concatenate x3 -> x0, other arithmetic: 4.83 us -> none  [the longest x1 3.26 us: on_device(): padded = jnp.concatenate([above, tile, below], axis=2)]
    unnamed x8, local copies, waits for them, and re-layouts: 1.7 us -> 5.49 us
  transfers between devices with their start and end apart: 3 -> 0, of which waited for: 3 -> 0; matrix products, arithmetic and copies ran while one was open for 2% -> 0% of each run, Pallas kernels for 0% -> 0%
where the time goes in v2:
time: 104 us; the launch traced here: 102 us
  Pallas kernels  95.8 us (92%)
  local copies, waits for them, and re-layouts  5.49 us (5%)
    pallas_call x1, Pallas kernels, compute(): pl.pallas_call(compute_kernel, name='llg', out_shape=[jax.ShapeDtypeStruc...  79.4 us
    pallas_call x1, Pallas kernels, gather_halo(): pl.pallas_call(halo_kernel, name='halo', out_shape=jax.ShapeDtypeStruct((...  16.4 us
    unnamed x8, local copies, waits for them, and re-layouts  5.49 us

profile of v2, /device:TPU:230, one launch (start us, length us, event | category | flops | bytes accessed | tf_op | source)
XLA Modules:
  0.0 101.9 jit_solution(10981610687294733978)
XLA Ops:
  0.6 0.0 copy-start.1
  0.6 1.1 %copy-done.1 = f32[3,4,64,256]{3,2,1,0:T(8,128)S(1)} copy-done((f32[3,4,64,256]{3,2,1,0:T(8,128)S(1)}, f32[3,4,64,256]{3,2,1,0:T(8,128)}, u32[]{:S(2)}) %copy-start.1) | copy-done | bytes 786456
  1.8 0.0 copy-start.2
  1.8 1.1 %copy-done.2 = f32[3,4,64,256]{3,2,1,0:T(8,128)S(1)} copy-done((f32[3,4,64,256]{3,2,1,0:T(8,128)S(1)}, f32[3,4,64,256]{3,2,1,0:T(8,128)}, u32[]{:S(2)}) %copy-start.2) | copy-done | bytes 786456
  2.9 0.0 copy-start.3
  2.9 0.9 copy-done.3
  3.9 16.4 %halo.1.fields = f32[7,4,5,72,128]{4,3,2,1,0:T(8,128)S(1)} custom-call(f32[3,4,64,256]{3,2,1,0:T(8,128)S(1)} %copy-done.1, f32[3,4,64,256]{3,2,1,0:T(8,128)S(1)} %copy-done.2, s32[4,64,256]{2,1,0:T(8,128)S(1)} %copy-done.3), custom_call_target="tpu_custom_call" | custom-call | tf_op jit(solution)/shard_map/halo/pallas_call | solution.py:420
  20.2 0.0 copy-start
  20.2 2.3 %copy-done = f32[7,4,5,72,128]{4,3,2,1,0:T(8,128)} copy-done((f32[7,4,5,72,128]{4,3,2,1,0:T(8,128)}, f32[7,4,5,72,128]{4,3,2,1,0:T(8,128)S(1)}, u32[]{:S(2)}) %copy-start) | copy-done | bytes 5160984
  22.5 79.4 %llg.1 = (f32[3,4,64,256]{3,2,1,0:T(8,128)}, f32[3,4,64,256]{3,2,1,0:T(8,128)}) custom-call(s32[1]{0:T(128)} %bitcast.index_ref, f32[4,3]{1,0:T(4,128)} %table.1, f32[7,4,5,72,128]{4,3,2,1,0:T(8,128)} %copy-done), custom_call_target="tpu_custom_call" | custom-call | tf_op jit(solution)/shard_map/llg/pallas_call | solution.py:289
Async XLA Ops:
  0.6 1.1 %copy-start.1 = (f32[3,4,64,256]{3,2,1,0:T(8,128)S(1)}, f32[3,4,64,256]{3,2,1,0:T(8,128)}, u32[]{:S(2)}) copy-start(f32[3,4,64,256]{3,2,1,0:T(8,128)} %start_ref.1) | copy-start | bytes 2359300
  1.8 1.1 %copy-start.2 = (f32[3,4,64,256]{3,2,1,0:T(8,128)S(1)}, f32[3,4,64,256]{3,2,1,0:T(8,128)}, u32[]{:S(2)}) copy-start(f32[3,4,64,256]{3,2,1,0:T(8,128)} %demag_ref.1) | copy-start | bytes 2359300
  2.9 0.9 copy-start.3
  20.2 2.3 %copy-start = (f32[7,4,5,72,128]{4,3,2,1,0:T(8,128)}, f32[7,4,5,72,128]{4,3,2,1,0:T(8,128)S(1)}, u32[]{:S(2)}) copy-start(f32[7,4,5,72,128]{4,3,2,1,0:T(8,128)S(1)} %halo.1.fields) | copy-start | bytes 15482884

commit v3 on v2

v3 whole, which is shorter than its diff:
```python
import jax
import jax.numpy as jnp
from jax import lax
from jax.experimental import pallas as pl
from jax.experimental.pallas import tpu as pltpu
from jax.sharding import PartitionSpec as P

MESH = pl.DeviceIdType.MESH
ITERS = 4
HALO = 24
SIDE = 32
STEP = 0.05
DEPTH = 8
FIRST = 8
LAST = 64
ROWS = 72
PARTS = 5


def blocks_of(halo):
    return (FIRST + HALO - halo) // 8, LAST // 8


def lanes():
    return lax.broadcasted_iota(jnp.int32, (8, 128), 1)


def neighbours(field, c, z, row):
    rows = pl.ds(row, 8)
    lane = lanes()
    first, last = lane == 0, lane == 127
    v = [field[c, z, part, rows, :] for part in range(PARTS)]
    n0, n2, n4 = (pltpu.roll(v[part], 127, 1) for part in (0, 2, 4))
    p1, p3, p4 = (pltpu.roll(v[part], 1, 1) for part in (1, 3, 4))
    ahead = pltpu.roll(jnp.where(lane == 32, v[4], v[2]), 95, 1)
    behind = pltpu.roll(jnp.where(lane == 95, v[4], v[3]), 33, 1)
    following = [
        v[1],
        jnp.where(last, n4, n0),
        v[3],
        jnp.where(last, ahead, n2),
        jnp.where(last, n0, jnp.where(lane == 95, ahead, n4)),
    ]
    previous = [
        jnp.where(first, p4, p1),
        v[0],
        jnp.where(first, behind, p3),
        v[2],
        jnp.where(first, p1, jnp.where(lane == 32, behind, p4)),
    ]
    return following, previous


def join_halves(field):
    lane = lax.broadcasted_iota(jnp.int32, (1, 128), 1)
    down = (lane < 32) | ((lane >= 64) & (lane < 96))
    edge, beyond = pl.ds(LAST - 1, 1), pl.ds(LAST, 1)
    for c in range(3):
        for z in range(4):
            for part in range(4):
                field[c, z, part, beyond, :] = field[c, z, (part + 2) % 4, edge, :]
            side = field[c, z, 4, edge, :]
            field[c, z, 4, beyond, :] = jnp.where(down, pltpu.roll(side, 96, 1), pltpu.roll(side, 32, 1))


def rates(field, aux, row, part, z, following, previous):
    exchange_ref, slope_ref, signed_ref, axis_ref, demag_ref = aux
    rows = pl.ds(row, 8)
    above = pl.ds(row - 1, 8)
    below = pl.ds(row + 1, 8)
    sums = []
    slope_x = [None] * 3
    center = [field[c, z, part, rows, :] for c in range(3)]
    for c in range(3):
        x_next = field[c, z, part, below, :]
        x_prev = field[c, z, part, above, :]
        if z in (0, 3):
            z_pair = field[c, 1 if z == 0 else 2, part, rows, :]
        else:
            z_pair = field[c, z + 1, part, rows, :] + field[c, z - 1, part, rows, :]
        sums.append((x_next + x_prev) + (following[c][part] + previous[c][part]) + z_pair)
        if c != 1:
            slope_x[c] = x_next - x_prev
    mx, my, mz = center
    own = 5.0 if z in (0, 3) else 6.0
    exchange = exchange_ref[z, part, rows, :]
    slope = slope_ref[z, part, rows, :]
    signed = signed_ref[z, part, rows, :]
    axis = axis_ref[z, part, rows, :]
    hx = exchange * (sums[0] - own * mx) + signed * slope_x[2] + demag_ref[0, z, part, rows, :]
    hy = (exchange * (sums[1] - own * my) + slope * (following[2][part] - previous[2][part])
          + demag_ref[1, z, part, rows, :])
    hz = (exchange * sums[2] + axis * mz
          - (signed * slope_x[0] + slope * (following[1][part] - previous[1][part])) + demag_ref[2, z, part, rows, :])
    gx = hx + (my * hz - mz * hy)
    gy = hy + (mz * hx - mx * hz)
    gz = hz + (mx * hy - my * hx)
    return (gy * mz - gz * my, gz * mx - gx * mz, gx * my - gy * mx), center


def put(ref, lead, z, part, row, values):
    for c in range(3):
        ref[(*lead, c, z, part, pl.ds(row, 8), slice(None))] = values[c]


def get(ref, lead, z, part, row):
    return [ref[(*lead, c, z, part, pl.ds(row, 8), slice(None))] for c in range(3)]


def evaluate(field, aux, halo, use):
    first, last = blocks_of(halo)
    join_halves(field)

    def run(block, carry):
        row = pl.multiple_of(block * 8, 8)
        for z in range(4):
            both = [neighbours(field, c, z, row) for c in range(3)]
            following, previous = [pair[0] for pair in both], [pair[1] for pair in both]
            for part in range(PARTS):
                out, cells = rates(field, aux, row, part, z, following, previous)
                use(row, part, z, out, cells)
        return carry

    pairs = (last - first) // 2

    def two(pair, carry):
        return run(first + 2 * pair + 1, run(first + 2 * pair, carry))

    lax.fori_loop(0, pairs, two, 0)
    lax.fori_loop(first + 2 * pairs, last, run, 0)


def permuted(values, permutation):
    high = values.astype(jnp.bfloat16)
    rest = values - high.astype(jnp.float32)
    middle = rest.astype(jnp.bfloat16)
    low = (rest - middle.astype(jnp.float32)).astype(jnp.bfloat16)
    product = jnp.dot(jnp.concatenate([high, middle, low], axis=0), permutation, preferred_element_type=jnp.float32)
    count = values.shape[0]
    return (product[:count] + product[count:2 * count]) + product[2 * count:]


def spread(natural_axis):
    natural = lax.broadcasted_iota(jnp.int32, (256, 256), natural_axis)
    sorted_at = lax.broadcasted_iota(jnp.int32, (256, 256), 1 - natural_axis)
    source = jnp.where(sorted_at < 128, 2 * sorted_at, 2 * sorted_at - 255)
    return (natural == source).astype(jnp.float32).astype(jnp.bfloat16)


def assemble(field, out_ref, order_ref):
    upside_down = 7 - lax.broadcasted_iota(jnp.int32, (8, 128), 0)
    inner = pl.ds(FIRST + HALO, 32)

    def body(z, carry):
        for c in range(3):
            sorted_rows = jnp.concatenate(
                [jnp.concatenate([field[c, z, part, inner, :], field[c, z, part + 1, inner, :]], axis=1) for part in (0, 2)],
                axis=0)
            rows = 2.0 * permuted(sorted_rows, order_ref[...])
            out_ref[c, z, 0:32, :] = rows[:32]
            for block in range(4):
                for columns in (slice(0, 128), slice(128, 256)):
                    out_ref[c, z, 32 + 8 * block:40 + 8 * block, columns] = jnp.take_along_axis(
                        rows[56 - 8 * block:64 - 8 * block, columns], upside_down, axis=0)
        return carry

    lax.fori_loop(0, 4, body, 0)


def fill_coefficients(table, region, exchange_ref, slope_ref, signed_ref, axis_ref):
    lane = lanes()
    upper_side = (lane < 32) | (lane >= 96)

    def body(block, carry):
        rows = pl.ds(pl.multiple_of(block * 8, 8), 8)
        for z in range(4):
            for part in range(PARTS):
                kind = region[z, part, rows, :]
                exchange, slope, axis = (
                    jnp.where(kind == 0.0, table[0, k], jnp.where(kind == 1.0, table[1, k], jnp.where(
                        kind == 2.0, table[2, k], table[3, k]))) for k in range(3))
                exchange = (2.0 * STEP) * exchange
                slope = STEP * slope
                exchange_ref[z, part, rows, :] = exchange
                slope_ref[z, part, rows, :] = slope
                signed_ref[z, part, rows, :] = (
                    slope if part < 2 else -slope if part < 4 else jnp.where(upper_side, slope, -slope))
                axis_ref[z, part, rows, :] = (4.0 * STEP) * axis - (5.0 if z in (0, 3) else 6.0) * exchange
        return carry

    lax.fori_loop(FIRST // 8, LAST // 8, body, 0)


def halve(refs):
    def body(block, carry):
        rows = pl.ds(pl.multiple_of(block * 8, 8), 8)
        for ref in refs:
            for z in range(4):
                for part in range(PARTS):
                    for lead in ((),) if len(ref.shape) == 4 else ((0,), (1,), (2,)):
                        at = (*lead, z, part, rows, slice(None))
                        ref[at] = 0.5 * ref[at]
        return carry

    lax.fori_loop(blocks_of(DEPTH - 1)[0], LAST // 8, body, 0)


def compute_kernel(index_ref, table, fields, end_ref, guess_ref,
                   state_even, state_odd, node_one, extra, rate_zero, rate_one, rate_two, node_two,
                   demag_ref, region, exchange_ref, slope_ref, signed_ref, axis_ref, order_ref, sems):
    me = index_ref[0]
    aux = (exchange_ref, slope_ref, signed_ref, axis_ref, demag_ref)
    loads = [
        pltpu.make_async_copy(fields.at[6], region, sems.at[0]),
        pltpu.make_async_copy(fields.at[0:3], state_even, sems.at[1]),
        pltpu.make_async_copy(fields.at[3:6], demag_ref, sems.at[2]),
    ]
    for copy in loads:
        copy.start()
    order_ref[...] = spread(1)
    loads[0].wait()
    fill_coefficients(table, region, exchange_ref, slope_ref, signed_ref, axis_ref)
    loads[1].wait()
    loads[2].wait()

    def load_start(target):
        copy = pltpu.make_async_copy(fields.at[0:3], target, sems.at[3])
        copy.start()
        copy.wait()

    def step_from(source, target, step):
        halo = me - step + DEPTH - 1

        @pl.when(step < me - 3)
        def _():
            def use(row, part, z, out, cells):
                put(target, (), z, part, row, [cells[c] + out[c] for c in range(3)])

            evaluate(source, aux, halo, use)

        @pl.when(step >= me - 3)
        def _():
            kept = step - me + 3

            def use(row, part, z, out, cells):
                half = [0.5 * out[c] for c in range(3)]
                put(target, (), z, part, row, [cells[c] + out[c] for c in range(3)])
                put(rate_zero, (kept,), z, part, row, half)
                put(node_one, (kept,), z, part, row, [cells[c] + half[c] for c in range(3)])

            evaluate(source, aux, halo, use)

    def advance(step, carry):
        even = lax.rem(step, 2) == 0
        pl.when(even)(lambda: step_from(state_even, state_odd, step))
        pl.when(jnp.logical_not(even))(lambda: step_from(state_odd, state_even, step))
        return carry

    lax.fori_loop(0, me + 1, advance, 0)
    halve(aux)
    pl.when(lax.rem(me, 2) == 0)(lambda: assemble(state_even, guess_ref, order_ref))
    pl.when(lax.rem(me, 2) == 1)(lambda: assemble(state_odd, guess_ref, order_ref))

    def sweep_slices(sweep, carry):
        halo = DEPTH - 2 - 2 * sweep

        def one_slice(count, carry):
            kept = 3 - count

            @pl.when((me - count >= 0) & (sweep == 0))
            def _():
                def use(row, part, z, out, cells):
                    put(node_two, (), z, part, row, [cells[c] + out[c] for c in range(3)])
                    put(rate_one, (kept,), z, part, row, out)

                evaluate(node_one.at[kept], aux, halo, use)

            @pl.when((me - count >= 0) & (sweep > 0))
            def _():
                def use(row, part, z, out, cells):
                    add = get(extra, (kept - 1,), z, part, row)
                    put(node_two, (), z, part, row, [cells[c] + out[c] + add[c] for c in range(3)])
                    put(rate_one, (kept,), z, part, row, out)

                evaluate(node_one.at[kept], aux, halo, use)

            pl.when((me - count == -1) & (sweep + 1 < ITERS))(lambda: load_start(node_two))

            @pl.when((count == 0) & (sweep + 1 < ITERS))
            def _():
                def use(row, part, z, out, cells):
                    put(rate_two, (), z, part, row, out)

                evaluate(node_two, aux, halo - 1, use)

            @pl.when((count > 0) & (me - count >= -1) & (sweep + 1 < ITERS))
            def _():
                def use(row, part, z, out, cells):
                    old = get(rate_zero, (kept + 1,), z, part, row)
                    mid = get(rate_one, (kept + 1,), z, part, row)
                    far = get(rate_two, (), z, part, row)
                    put(node_one, (kept + 1,), z, part, row, [
                        cells[c] + out[c] + (1.0 / 12.0) * (8.0 * mid[c] - 7.0 * old[c] - far[c])
                        for c in range(3)])
                    put(extra, (kept,), z, part, row, [
                        (1.0 / 12.0) * ((far[c] - old[c]) + 4.0 * (far[c] - mid[c]))
                        for c in range(3)])
                    put(rate_zero, (kept + 1,), z, part, row, out)
                    put(rate_two, (), z, part, row, out)

                evaluate(node_two, aux, halo - 1, use)

            return carry

        return lax.fori_loop(0, ITERS - sweep, one_slice, carry)

    lax.fori_loop(0, ITERS, sweep_slices, 0)
    assemble(node_two, end_ref, order_ref)


def compute(index, table, fields, interpret=False):
    field = (3, 4, PARTS, ROWS, 128)
    vmem = pl.BlockSpec(memory_space=pltpu.VMEM)
    smem = pl.BlockSpec(memory_space=pltpu.SMEM)
    return pl.pallas_call(
        compute_kernel,
        name="llg",
        out_shape=[jax.ShapeDtypeStruct((3, 4, 64, 256), jnp.float32)] * 2,
        in_specs=[smem, smem, pl.BlockSpec(memory_space=pltpu.HBM)],
        out_specs=[vmem] * 2,
        scratch_shapes=[
            pltpu.VMEM(field, jnp.float32),
            pltpu.VMEM(field, jnp.float32),
            pltpu.VMEM((4,) + field, jnp.float32),
            pltpu.VMEM((3,) + field, jnp.float32),
            pltpu.VMEM((4,) + field, jnp.float32),
            pltpu.VMEM((4,) + field, jnp.float32),
            pltpu.VMEM(field, jnp.float32),
            pltpu.VMEM(field, jnp.float32),
            pltpu.VMEM(field, jnp.float32),
        ] + [pltpu.VMEM(field[1:], jnp.float32)] * 5 + [
            pltpu.VMEM((256, 256), jnp.bfloat16), pltpu.SemaphoreType.DMA((4,))],
        compiler_params=pltpu.CompilerParams(vmem_limit_bytes=62 * 1024 * 1024),
        interpret=interpret,
    )(index, table, fields)


def halo_kernel(start_hbm, demag_hbm, region_hbm, out_ref, start_ref, demag_ref, region_ref, order_ref, own, down, up, side_out, side_in, corner_out, corner_in, corner,
                send_sems, recv_sems, local_sems):
    gx, gy, tm = lax.axis_index("gx"), lax.axis_index("gy"), lax.axis_index("tm")
    count = lax.axis_size("gx")
    after = {"gx": lax.rem(gx + 1, count)}
    before = {"gx": lax.rem(gx + count - 1, count)}
    across = {"tm": tm + 1 - 2 * lax.rem(tm, 2), "gy": 1 - gy}
    loads = [pltpu.make_async_copy(source, target, local_sems.at[3 + k]) for k, (source, target) in enumerate(
        ((start_hbm, start_ref), (demag_hbm, demag_ref), (region_hbm, region_ref)))]
    for copy in loads:
        copy.start()
    barrier = pltpu.get_barrier_semaphore()
    for device in (after, before, across):
        pl.semaphore_signal(barrier, inc=1, device_id=device, device_id_type=MESH)

    upside_down = 7 - lax.broadcasted_iota(jnp.int32, (8, 128), 0)
    lane = lanes()

    def flip(value):
        return jnp.take_along_axis(value, upside_down, axis=0)

    def load(f, z):
        if f < 3:
            return 0.5 * start_ref[f, z]
        if f < 6:
            return STEP * demag_ref[f - 3, z]
        return region_ref[z].astype(jnp.float32)

    def quarters(a, b, c, d):
        return jnp.where(lane < 64, jnp.where(lane < 32, a, b), jnp.where(lane < 96, c, d))

    def piece(values, row, part):
        return values[row:row + 8, 128 * part:128 * part + 128]

    def stage_sides(z, carry):
        for f in range(7):
            tile = load(f, z)
            for k in range(4):
                a = [piece(tile, 8 * k, part) for part in range(2)]
                b = [flip(piece(tile, 56 - 8 * k, part)) for part in range(2)]
                side_out[f, z, 8 * k:8 * k + 8, :] = quarters(a[0], pltpu.roll(b[0], 32, 1), pltpu.roll(b[1], 96, 1), a[1])
        return carry

    def stage_rows(z, carry):
        for f in range(7):
            tile = load(f, z)
            if f < 6:
                halves = permuted(tile, order_ref[...])
            else:
                halves = jnp.dot(tile.astype(jnp.bfloat16), order_ref[...], preferred_element_type=jnp.float32)
            for k in range(4):
                rows = slice(8 * k, 8 * k + 8)
                for part in range(2):
                    own[f, z, part, rows, :] = piece(halves, 8 * k, part)
                    own[f, z, part + 2, rows, :] = flip(piece(halves, 56 - 8 * k, part))
            for k in range(3):
                rows = slice(8 * k, 8 * k + 8)
                for part in range(2):
                    down[f, z, part, rows, :] = piece(halves, 40 + 8 * k, part)
                    up[f, z, part, rows, :] = flip(piece(halves, 16 - 8 * k, part))
        return carry

    def send(number, source, target, device):
        copy = pltpu.make_async_remote_copy(source, target, send_sems.at[number], recv_sems.at[number],
                                            device_id=device, device_id_type=MESH)
        copy.start()
        return copy

    for copy in loads:
        copy.wait()
    lax.fori_loop(0, 4, stage_sides, 0)
    pl.semaphore_wait(barrier, 3)
    near, far = slice(0, HALO), slice(HALO, 32)
    sides = [send(k, side_out.at[:, :, rows, :], side_in.at[:, :, rows, :], across) for k, rows in enumerate((near, far))]
    order_ref[...] = spread(0)
    lax.fori_loop(0, 4, stage_rows, 0)
    edge, inner = slice(FIRST, FIRST + HALO), slice(FIRST + HALO, LAST)
    edges = [send(2, down, out_ref.at[:, :, 0:2, edge, :], after), send(3, up, out_ref.at[:, :, 2:4, edge, :], before)]
    middle = pltpu.make_async_copy(own, out_ref.at[:, :, 0:4, inner, :], local_sems.at[0])
    middle.start()
    sides[0].wait_recv()

    def turn(pair, carry):
        for f in range(7):
            for k in range(3):
                rows = slice(8 * k, 8 * k + 8)
                back = slice(16 - 8 * k, 24 - 8 * k)
                one = flip(side_in[f, pair, back, :])
                two = flip(side_in[f, pair + 2, back, :])
                one_left, one_right = pltpu.roll(one, 96, 1), pltpu.roll(one, 32, 1)
                two_left, two_right = pltpu.roll(two, 96, 1), pltpu.roll(two, 32, 1)
                corner_out[0, f, pair, rows, :] = quarters(one_left, two_left, two_right, one_right)
                corner_out[1, f, pair, rows, :] = quarters(two_right, one_right, one_left, two_left)
        return carry

    lax.fori_loop(0, 2, turn, 0)
    corners = [send(4, corner_out.at[0], corner_in.at[0], after), send(5, corner_out.at[1], corner_in.at[1], before)]
    sides[1].wait_recv()
    strip = pltpu.make_async_copy(side_in, out_ref.at[:, :, 4, inner, :], local_sems.at[1])
    strip.start()
    corners[0].wait_recv()
    corners[1].wait_recv()
    mid = (lane >= 32) & (lane < 96)

    def unpack(pair, carry):
        for f in range(7):
            for k in range(3):
                rows = slice(8 * k, 8 * k + 8)
                upper, lower = corner_in[0, f, pair, rows, :], corner_in[1, f, pair, rows, :]
                corner[f, pair, rows, :] = jnp.where(mid, lower, upper)
                corner[f, pair + 2, rows, :] = pltpu.roll(jnp.where(mid, upper, lower), 64, 1)
        return carry

    lax.fori_loop(0, 2, unpack, 0)
    last = pltpu.make_async_copy(corner, out_ref.at[:, :, 4, edge, :], local_sems.at[2])
    last.start()
    for copy in edges:
        copy.wait()
    for copy in sides + corners:
        copy.wait_send()
    middle.wait()
    strip.wait()
    last.wait()


def gather_halo(start_field, demag_field, region_map):
    hbm = pl.BlockSpec(memory_space=pltpu.HBM)
    return pl.pallas_call(
        halo_kernel,
        name="halo",
        out_shape=jax.ShapeDtypeStruct((7, 4, PARTS, ROWS, 128), jnp.float32),
        in_specs=[hbm] * 3,
        out_specs=hbm,
        scratch_shapes=[
            pltpu.VMEM((3, 4, 64, 256), jnp.float32),
            pltpu.VMEM((3, 4, 64, 256), jnp.float32),
            pltpu.VMEM((4, 64, 256), jnp.int32),
            pltpu.VMEM((256, 256), jnp.bfloat16),
            pltpu.VMEM((7, 4, 4, 32, 128), jnp.float32),
            pltpu.VMEM((7, 4, 2, HALO, 128), jnp.float32),
            pltpu.VMEM((7, 4, 2, HALO, 128), jnp.float32),
            pltpu.VMEM((7, 4, 32, 128), jnp.float32),
            pltpu.VMEM((7, 4, 32, 128), jnp.float32),
            pltpu.VMEM((2, 7, 2, HALO, 128), jnp.float32),
            pltpu.VMEM((2, 7, 2, HALO, 128), jnp.float32),
            pltpu.VMEM((7, 4, HALO, 128), jnp.float32),
            pltpu.SemaphoreType.DMA((6,)),
            pltpu.SemaphoreType.DMA((6,)),
            pltpu.SemaphoreType.DMA((6,)),
        ],
        compiler_params=pltpu.CompilerParams(
            collective_id=0, has_side_effects=True, vmem_limit_bytes=62 * 1024 * 1024),
    )(start_field, demag_field, region_map)


def on_device(start_field, demag_field, region_map, material_table):
    fields = gather_halo(start_field, demag_field, region_map)
    index = lax.axis_index("tm").astype(jnp.int32)[None]
    end, guess = compute(index, material_table, fields)
    return end[None], guess[None]


def solution(mesh):
    placed = (P(None, None, "gx", "gy"), P(None, None, "gx", "gy"), P(None, "gx", "gy"), P())
    return jax.shard_map(
        on_device,
        mesh=mesh,
        in_specs=placed,
        out_specs=(P("tm", None, None, "gx", "gy"), P("tm", None, None, "gx", "gy")),
        check_vma=False,
    )
```

time: 104 us -> 80.3 us (0.77)
  Pallas kernels: 95.8 us -> 78.1 us
  local copies, waits for them, and re-layouts: 5.49 us -> 0 us
    pallas_call x1, Pallas kernels: 79.4 us -> 60.5 us  [compute(): pl.pallas_call(compute_kernel, name='llg', out_shape=[jax.ShapeDtypeStruc...]
    unnamed x8 -> x0, local copies, waits for them, and re-layouts: 5.49 us -> none
    pallas_call x1, Pallas kernels: 16.4 us -> 17.5 us  [gather_halo(): pl.pallas_call(halo_kernel, name='halo', out_shape=jax.ShapeDtypeStruct((...]
where the time goes in v3:
time: 80.3 us; the launch traced here: 78.7 us
  Pallas kernels  78.1 us (97%)
    pallas_call x1, Pallas kernels, compute(): pl.pallas_call(compute_kernel, name='llg', out_shape=[jax.ShapeDtypeStruc...  60.5 us
    pallas_call x1, Pallas kernels, gather_halo(): pl.pallas_call(halo_kernel, name='halo', out_shape=jax.ShapeDtypeStruct((...  17.5 us

profile of v3, /device:TPU:230, one launch (start us, length us, event | category | flops | bytes accessed | tf_op | source)
XLA Modules:
  0.0 78.7 jit_solution(13916474329061451610)
XLA Ops:
  0.6 17.5 %halo.1.fields = f32[7,4,5,72,128]{4,3,2,1,0:T(8,128)} custom-call(f32[3,4,64,256]{3,2,1,0:T(8,128)} %start_hbm.1, f32[3,4,64,256]{3,2,1,0:T(8,128)} %demag_hbm.1, s32[4,64,256]{2,1,0:T(8,128)} %region_hbm.1), custom_call_target="tpu_custom_call" | custom-call | tf_op jit(solution)/shard_map/halo/pallas_call | solution.py:475
  18.2 60.5 %llg.1 = (f32[3,4,64,256]{3,2,1,0:T(8,128)}, f32[3,4,64,256]{3,2,1,0:T(8,128)}) custom-call(s32[1]{0:T(128)} %bitcast.index_ref, f32[4,3]{1,0:T(4,128)} %table.1, f32[7,4,5,72,128]{4,3,2,1,0:T(8,128)} %halo.1.fields), custom_call_target="tpu_custom_call" | custom-call | tf_op jit(solution)/shard_map/llg/pallas_call | solution.py:325

commit v4 on v3

--- a/solution.py
+++ b/solution.py
@@ -147,7 +147,7 @@
     return (natural == source).astype(jnp.float32).astype(jnp.bfloat16)
 
 
-def assemble(field, out_ref, order_ref):
+def assemble(field, out_ref, out_hbm, sem, order_ref):
     upside_down = 7 - lax.broadcasted_iota(jnp.int32, (8, 128), 0)
     inner = pl.ds(FIRST + HALO, 32)
 
@@ -162,6 +162,7 @@
                 for columns in (slice(0, 128), slice(128, 256)):
                     out_ref[c, z, 32 + 8 * block:40 + 8 * block, columns] = jnp.take_along_axis(
                         rows[56 - 8 * block:64 - 8 * block, columns], upside_down, axis=0)
+        pltpu.make_async_copy(out_ref.at[:, z], out_hbm.at[:, z], sem).start()
         return carry
 
     lax.fori_loop(0, 4, body, 0)
@@ -205,7 +206,7 @@
     lax.fori_loop(blocks_of(DEPTH - 1)[0], LAST // 8, body, 0)
 
 
-def compute_kernel(index_ref, table, fields, end_ref, guess_ref,
+def compute_kernel(index_ref, table, fields, end_hbm, guess_hbm, end_ref, guess_ref,
                    state_even, state_odd, node_one, extra, rate_zero, rate_one, rate_two, node_two,
                    demag_ref, region, exchange_ref, slope_ref, signed_ref, axis_ref, order_ref, sems):
     me = index_ref[0]
@@ -258,8 +259,8 @@
 
     lax.fori_loop(0, me + 1, advance, 0)
     halve(aux)
-    pl.when(lax.rem(me, 2) == 0)(lambda: assemble(state_even, guess_ref, order_ref))
-    pl.when(lax.rem(me, 2) == 1)(lambda: assemble(state_odd, guess_ref, order_ref))
+    pl.when(lax.rem(me, 2) == 0)(lambda: assemble(state_even, guess_ref, guess_hbm, sems.at[4], order_ref))
+    pl.when(lax.rem(me, 2) == 1)(lambda: assemble(state_odd, guess_ref, guess_hbm, sems.at[4], order_ref))
 
     def sweep_slices(sweep, carry):
         halo = DEPTH - 2 - 2 * sweep
@@ -315,20 +316,23 @@
         return lax.fori_loop(0, ITERS - sweep, one_slice, carry)
 
     lax.fori_loop(0, ITERS, sweep_slices, 0)
-    assemble(node_two, end_ref, order_ref)
+    assemble(node_two, end_ref, end_hbm, sems.at[5], order_ref)
+    pltpu.make_async_copy(guess_ref, guess_hbm, sems.at[4]).wait()
+    pltpu.make_async_copy(end_ref, end_hbm, sems.at[5]).wait()
 
 
 def compute(index, table, fields, interpret=False):
     field = (3, 4, PARTS, ROWS, 128)
-    vmem = pl.BlockSpec(memory_space=pltpu.VMEM)
     smem = pl.BlockSpec(memory_space=pltpu.SMEM)
     return pl.pallas_call(
         compute_kernel,
         name="llg",
         out_shape=[jax.ShapeDtypeStruct((3, 4, 64, 256), jnp.float32)] * 2,
         in_specs=[smem, smem, pl.BlockSpec(memory_space=pltpu.HBM)],
-        out_specs=[vmem] * 2,
+        out_specs=[pl.BlockSpec(memory_space=pltpu.HBM)] * 2,
         scratch_shapes=[
+            pltpu.VMEM((3, 4, 64, 256), jnp.float32),
+            pltpu.VMEM((3, 4, 64, 256), jnp.float32),
             pltpu.VMEM(field, jnp.float32),
             pltpu.VMEM(field, jnp.float32),
             pltpu.VMEM((4,) + field, jnp.float32),
@@ -339,7 +343,7 @@
             pltpu.VMEM(field, jnp.float32),
             pltpu.VMEM(field, jnp.float32),
         ] + [pltpu.VMEM(field[1:], jnp.float32)] * 5 + [
-            pltpu.VMEM((256, 256), jnp.bfloat16), pltpu.SemaphoreType.DMA((4,))],
+            pltpu.VMEM((256, 256), jnp.bfloat16), pltpu.SemaphoreType.DMA((6,))],
         compiler_params=pltpu.CompilerParams(vmem_limit_bytes=62 * 1024 * 1024),
         interpret=interpret,
     )(index, table, fields)
@@ -418,7 +422,7 @@
     lax.fori_loop(0, 4, stage_sides, 0)
     pl.semaphore_wait(barrier, 3)
     near, far = slice(0, HALO), slice(HALO, 32)
-    sides = [send(k, side_out.at[:, :, rows, :], side_in.at[:, :, rows, :], across) for k, rows in enumerate((near, far))]
+    sides = [send(0, side_out.at[:, :, near, :], side_in.at[:, :, near, :], across)]
     order_ref[...] = spread(0)
     lax.fori_loop(0, 4, stage_rows, 0)
     edge, inner = slice(FIRST, FIRST + HALO), slice(FIRST + HALO, LAST)
@@ -426,6 +430,7 @@
     middle = pltpu.make_async_copy(own, out_ref.at[:, :, 0:4, inner, :], local_sems.at[0])
     middle.start()
     sides[0].wait_recv()
+    sides.append(send(1, side_out.at[:, :, far, :], side_in.at[:, :, far, :], across))
 
     def turn(pair, carry):
         for f in range(7):

time: 80.3 us -> 79.5 us (0.990)
  no operation moved by 1% of the time
where the time goes in v4:
time: 79.5 us; the launch traced here: 78.5 us
  Pallas kernels  77.9 us (98%)
    pallas_call x1, Pallas kernels, compute(): pl.pallas_call(compute_kernel, name='llg', out_shape=[jax.ShapeDtypeStruc...  60.3 us
    pallas_call x1, Pallas kernels, gather_halo(): pl.pallas_call(halo_kernel, name='halo', out_shape=jax.ShapeDtypeStruct((...  17.5 us

profile of v4, /device:TPU:230, one launch (start us, length us, event | category | flops | bytes accessed | tf_op | source)
XLA Modules:
  0.0 78.5 jit_solution(11794549358411361930)
XLA Ops:
  0.6 17.5 %halo.1.fields = f32[7,4,5,72,128]{4,3,2,1,0:T(8,128)} custom-call(f32[3,4,64,256]{3,2,1,0:T(8,128)} %start_hbm.1, f32[3,4,64,256]{3,2,1,0:T(8,128)} %demag_hbm.1, s32[4,64,256]{2,1,0:T(8,128)} %region_hbm.1), custom_call_target="tpu_custom_call" | custom-call | tf_op jit(solution)/shard_map/halo/pallas_call | solution.py:480
  18.2 60.3 %llg.1 = (f32[3,4,64,256]{3,2,1,0:T(8,128)}, f32[3,4,64,256]{3,2,1,0:T(8,128)}) custom-call(s32[1]{0:T(128)} %bitcast.index_ref, f32[4,3]{1,0:T(4,128)} %table.1, f32[7,4,5,72,128]{4,3,2,1,0:T(8,128)} %halo.1.fields), custom_call_target="tpu_custom_call" | custom-call | tf_op jit(solution)/shard_map/llg/pallas_call | solution.py:327
